TPU v7x, 32 devices: a whole 2x2x4 slice. The times are simulated.
32 devices in a mesh: ctx: 8 (over z, y), fsdp: 4 (over x, core).
Axes of the slice: x: 2, y: 2, z: 4, core: 2. Of those that a mesh axis runs over, the one named last changes fastest.
Arguments:
- tokens: bfloat16 [4, 4096, 1024], P('fsdp', 'ctx'), may hold values from -6 to 6
- block_pos: int32 [4, 16], P('fsdp'), may hold values from 0 to 15, each once within a row
- gain_attn: bfloat16 [1024], P('fsdp'), may hold values from 0.25 to 1.75
- w_query: bfloat16 [1024, 256], P('fsdp'), may hold values from -0.1875 to 0.1875
- w_key: bfloat16 [1024, 256], P('fsdp'), may hold values from -0.1875 to 0.1875
- w_value: bfloat16 [1024, 1024], P('fsdp'), may hold values from -0.1875 to 0.1875
- w_out: bfloat16 [1024, 1024], P('fsdp'), may hold values from -2 to 2
- gain_ffn: bfloat16 [1024], P('fsdp'), may hold values from 0.25 to 1.75
- w_gate: bfloat16 [1024, 2752], P('fsdp'), may hold values from -0.1875 to 0.1875
- w_up: bfloat16 [1024, 2752], P('fsdp'), may hold values from -0.1875 to 0.1875
- w_down: bfloat16 [2752, 1024], P('fsdp'), may hold values from -0.109375 to 0.109375
- cotangent: bfloat16 [4, 4096, 1024], P('fsdp', 'ctx'), may hold values from -6 to 6
Outputs:
- output: bfloat16 [4, 4096, 1024], P('fsdp', 'ctx')
- grad_tokens: float32 [4, 4096, 1024], P('fsdp', 'ctx')
- grad_gain_attn: float32 [1024], P('fsdp')
- grad_query: float32 [1024, 256], P('fsdp')
- grad_key: float32 [1024, 256], P('fsdp')
- grad_value: float32 [1024, 1024], P('fsdp')
- grad_out: float32 [1024, 1024], P('fsdp')
- grad_gain_ffn: float32 [1024], P('fsdp')
- grad_gate: float32 [1024, 2752], P('fsdp')
- grad_up: float32 [1024, 2752], P('fsdp')
- grad_down: float32 [2752, 1024], P('fsdp')
Inputs may be any that keep to these rules, and one draw needn't show every extreme that they name: `block_pos`: each row is a permutation of the 16 position blocks of one sequence.
All inputs are finite; a program needn't handle non-finite values.
Results may differ from a plain program's by a relative error of at most 0.015.
Values may be sent and summed in bfloat16 or wider, within the bound.
A program may use at most 512 MiB of HBM per device.

v0:
```python
import jax
import jax.numpy as jnp
from jax import lax
from jax.sharding import PartitionSpec as P

HEADS = 16
FDIM = 16
VDIM = 64
BLOCK = 256


highest = lax.Precision.HIGHEST
eps_norm = 1e-05
root_half = 0.7071067811865476


def features(scaled):
    outer_prod = scaled[..., :, None] * scaled[..., None, :]
    flattened = (
        outer_prod.reshape(scaled.shape[:-1] + (scaled.shape[-1] * scaled.shape[-1],)) * root_half
    )
    constant = jnp.ones(scaled.shape[:-1] + (1,), jnp.float32)
    return jnp.concatenate([constant, scaled, flattened], axis=-1)


def features_back(scaled, grad_feat):
    feat_dim = scaled.shape[-1]
    linear = grad_feat[..., 1 : 1 + feat_dim]
    square = (
        grad_feat[..., 1 + feat_dim :].reshape(scaled.shape[:-1] + (feat_dim, feat_dim)) * root_half
    )
    return linear + jnp.einsum("...ab,...b->...a", square + jnp.swapaxes(square, -1, -2), scaled)


def norm_forward(values, gain_vector):
    inv_rms = lax.rsqrt(jnp.mean(values * values, axis=-1, keepdims=True) + eps_norm)
    return (values * inv_rms * gain_vector, inv_rms)


def norm_backward(values, inv_rms, gain_vector, grad_normed):
    weighted = grad_normed * gain_vector
    grad_gain = jnp.sum(grad_normed * values * inv_rms, axis=0)
    grad_values = inv_rms * weighted - values * (inv_rms * inv_rms * inv_rms) * jnp.mean(
        weighted * values, axis=-1, keepdims=True
    )
    return (grad_values, grad_gain)


def block_group():
    for group_size in (8, 4, 2):
        return group_size
    return 1


def body(
    tokens,
    block_pos,
    gain_attn,
    w_query,
    w_key,
    w_value,
    w_out,
    gain_ffn,
    w_gate,
    w_up,
    w_down,
    cotangent,
):
    gathered = (
        lax.all_gather(gain_attn, "fsdp", axis=0, tiled=True),
        lax.all_gather(w_query, "fsdp", axis=0, tiled=True),
        lax.all_gather(w_key, "fsdp", axis=0, tiled=True),
        lax.all_gather(w_value, "fsdp", axis=0, tiled=True),
        lax.all_gather(w_out, "fsdp", axis=0, tiled=True),
        lax.all_gather(gain_ffn, "fsdp", axis=0, tiled=True),
        lax.all_gather(w_gate, "fsdp", axis=0, tiled=True),
        lax.all_gather(w_up, "fsdp", axis=0, tiled=True),
        lax.all_gather(w_down, "fsdp", axis=0, tiled=True),
    )
    norm_one_gain = gathered[0].astype(jnp.float32)
    query_full, key_full, value_full, out_full = (
        gathered[1],
        gathered[2],
        gathered[3],
        gathered[4],
    )
    norm_two_gain = gathered[5].astype(jnp.float32)
    gate_full, up_full, down_full = (gathered[6], gathered[7], gathered[8])
    residual = tokens[0].astype(jnp.float32)
    row_count = residual.shape[0]
    local_blocks = row_count // BLOCK
    feat_width = 1 + FDIM + FDIM * FDIM
    positions = block_pos[0]
    own_positions = lax.dynamic_slice_in_dim(
        positions, lax.axis_index("ctx") * local_blocks, local_blocks
    )
    normed_one, inv_rms_one = norm_forward(residual, norm_one_gain)
    normed_one_low = normed_one.astype(jnp.bfloat16)
    queries = jnp.dot(normed_one_low, query_full, preferred_element_type=jnp.float32).astype(
        jnp.bfloat16
    )
    keys_all = jnp.dot(normed_one_low, key_full, preferred_element_type=jnp.float32).astype(
        jnp.bfloat16
    )
    values_all = jnp.dot(normed_one_low, value_full, preferred_element_type=jnp.float32).astype(
        jnp.bfloat16
    )
    query_blocks = queries.reshape(local_blocks, BLOCK, HEADS, FDIM)
    key_blocks = keys_all.reshape(local_blocks, BLOCK, HEADS, FDIM)
    value_blocks = values_all.reshape(local_blocks, BLOCK, HEADS, VDIM)
    query_scaled = query_blocks.astype(jnp.float32) * 0.5
    key_scaled = key_blocks.astype(jnp.float32) * 0.5
    phi_query = features(query_scaled).astype(jnp.bfloat16)
    phi_key = features(key_scaled).astype(jnp.bfloat16)
    state_zero = jnp.zeros((local_blocks, HEADS, feat_width, VDIM), jnp.float32)
    norm_zero = jnp.zeros((local_blocks, HEADS, feat_width), jnp.float32)
    running = (state_zero, norm_zero)
    key_piece = lax.all_gather(keys_all, "ctx", axis=0, tiled=True)
    value_piece = lax.all_gather(values_all, "ctx", axis=0, tiled=True)
    block_count = key_piece.shape[0] // BLOCK
    group_size = block_group()
    others = positions
    key_groups = key_piece.reshape(block_count // group_size, group_size, BLOCK, HEADS, FDIM)
    value_groups = value_piece.reshape(block_count // group_size, group_size, BLOCK, HEADS, VDIM)
    other_groups = others.reshape(block_count // group_size, group_size)

    def one_group(inner_sum, group_args):
        keys_here, values_here, places = group_args
        key_feat = features(keys_here.astype(jnp.float32) * 0.5).astype(jnp.bfloat16)
        states = jnp.einsum(
            "gthf,gthv->ghfv", key_feat, values_here, preferred_element_type=jnp.float32
        )
        norm_sums = jnp.sum(key_feat.astype(jnp.float32), axis=1)
        earlier = (places[None, :] < own_positions[:, None]).astype(jnp.float32)
        return (
            (
                inner_sum[0] + jnp.einsum("ig,ghfv->ihfv", earlier, states, precision=highest),
                inner_sum[1] + jnp.einsum("ig,ghf->ihf", earlier, norm_sums, precision=highest),
            ),
            None,
        )

    running, unused = lax.scan(one_group, running, (key_groups, value_groups, other_groups))
    prefix, prefix_norm = running
    phi_query_wide = phi_query.astype(jnp.float32)
    scores = (
        jnp.einsum("nshf,nthf->nhst", query_blocks, key_blocks, preferred_element_type=jnp.float32)
        * 0.25
    )
    kernel = 1.0 + scores + 0.5 * scores * scores
    kernel_low = kernel.astype(jnp.bfloat16)
    numerator = jnp.einsum(
        "nhst,nthv->nshv", kernel_low, value_blocks, preferred_element_type=jnp.float32
    ) + jnp.einsum("nshf,nhfv->nshv", phi_query_wide, prefix, precision=highest)
    denominator = jnp.transpose(jnp.sum(kernel, axis=-1), (0, 2, 1)) + jnp.einsum(
        "nshf,nhf->nsh", phi_query_wide, prefix_norm, precision=highest
    )
    attention_full = numerator / denominator[..., None]
    attention_low = attention_full.reshape(row_count, HEADS * VDIM).astype(jnp.bfloat16)
    middle = residual + jnp.dot(attention_low, out_full, preferred_element_type=jnp.float32)
    normed_two, inv_rms_two = norm_forward(middle, norm_two_gain)
    normed_two_low = normed_two.astype(jnp.bfloat16)
    gate_pre = jnp.dot(normed_two_low, gate_full, preferred_element_type=jnp.float32)
    up_pre = jnp.dot(normed_two_low, up_full, preferred_element_type=jnp.float32)
    sigmoid_gate = jax.nn.sigmoid(gate_pre)
    silu_gate = gate_pre * sigmoid_gate
    hidden_low = (silu_gate * up_pre).astype(jnp.bfloat16)
    result = middle + jnp.dot(hidden_low, down_full, preferred_element_type=jnp.float32)
    output = result.astype(jnp.bfloat16)[None]
    cotangent_low = cotangent[0]
    grad_out_full = cotangent_low.astype(jnp.float32)
    grad_down_full = jnp.einsum(
        "tf,td->fd", hidden_low, cotangent_low, preferred_element_type=jnp.float32
    )
    grad_hidden = jnp.einsum(
        "td,fd->tf", cotangent_low, down_full, preferred_element_type=jnp.float32
    )
    grad_gate_pre = (
        grad_hidden * up_pre * (sigmoid_gate * (1.0 + gate_pre * (1.0 - sigmoid_gate)))
    ).astype(jnp.bfloat16)
    grad_up_pre = (grad_hidden * silu_gate).astype(jnp.bfloat16)
    grad_gate_full = jnp.einsum(
        "td,tf->df", normed_two_low, grad_gate_pre, preferred_element_type=jnp.float32
    )
    grad_up_full = jnp.einsum(
        "td,tf->df", normed_two_low, grad_up_pre, preferred_element_type=jnp.float32
    )
    grad_normed_two = jnp.einsum(
        "tf,df->td", grad_gate_pre, gate_full, preferred_element_type=jnp.float32
    ) + jnp.einsum("tf,df->td", grad_up_pre, up_full, preferred_element_type=jnp.float32)
    grad_middle_norm, grad_gain_two = norm_backward(
        middle, inv_rms_two, norm_two_gain, grad_normed_two
    )
    grad_middle = grad_out_full + grad_middle_norm
    grad_branch = grad_middle.astype(jnp.bfloat16)
    grad_out_proj = jnp.einsum(
        "ta,td->ad", attention_low, grad_branch, preferred_element_type=jnp.float32
    )
    grad_attention = jnp.einsum(
        "td,ad->ta", grad_branch, out_full, preferred_element_type=jnp.float32
    )
    grad_attention = grad_attention.reshape(local_blocks, BLOCK, HEADS, VDIM)
    grad_numerator = (grad_attention / denominator[..., None]).astype(jnp.bfloat16)
    grad_denominator = (-jnp.sum(grad_attention * attention_full, axis=-1) / denominator).astype(
        jnp.bfloat16
    )
    grad_denom_wide = grad_denominator.astype(jnp.float32)
    grad_kernel = (
        jnp.einsum(
            "nshv,nthv->nhst", grad_numerator, value_blocks, preferred_element_type=jnp.float32
        )
        + jnp.transpose(grad_denom_wide, (0, 2, 1))[..., None]
    )
    grad_scores = ((1.0 + scores) * grad_kernel).astype(jnp.bfloat16)
    flat_numer = grad_numerator.reshape(row_count, HEADS * VDIM)
    flat_denom = grad_denominator.reshape(row_count, HEADS)
    running = (state_zero, norm_zero)
    query_piece = lax.all_gather(queries, "ctx", axis=0, tiled=True)
    numer_piece = lax.all_gather(flat_numer, "ctx", axis=0, tiled=True)
    denom_piece = lax.all_gather(flat_denom, "ctx", axis=0, tiled=True)
    block_count = query_piece.shape[0] // BLOCK
    group_size = block_group()
    others = positions
    query_groups = query_piece.reshape(block_count // group_size, group_size, BLOCK, HEADS, FDIM)
    numer_groups = numer_piece.reshape(block_count // group_size, group_size, BLOCK, HEADS, VDIM)
    denom_groups = denom_piece.reshape(block_count // group_size, group_size, BLOCK, HEADS)
    other_groups = others.reshape(block_count // group_size, group_size)

    def one_group(inner_sum, group_args):
        queries_here, numer_here, denom_here, places = group_args
        query_feat = features(queries_here.astype(jnp.float32) * 0.5).astype(jnp.bfloat16)
        grad_states = jnp.einsum(
            "gthf,gthv->ghfv", query_feat, numer_here, preferred_element_type=jnp.float32
        )
        grad_norms = jnp.einsum(
            "gthf,gth->ghf", query_feat, denom_here, preferred_element_type=jnp.float32
        )
        later_mask = (places[None, :] > own_positions[:, None]).astype(jnp.float32)
        return (
            (
                inner_sum[0]
                + jnp.einsum("ig,ghfv->ihfv", later_mask, grad_states, precision=highest),
                inner_sum[1] + jnp.einsum("ig,ghf->ihf", later_mask, grad_norms, precision=highest),
            ),
            None,
        )

    running, unused = lax.scan(
        one_group, running, (query_groups, numer_groups, denom_groups, other_groups)
    )
    later_states, later_norms = running
    grad_phi_query = (
        jnp.einsum("nshv,nhfv->nshf", grad_numerator.astype(jnp.float32), prefix, precision=highest)
        + grad_denom_wide[..., None] * prefix_norm[:, None, :, :]
    )
    grad_phi_key = (
        jnp.einsum(
            "nthv,nhfv->nthf", value_blocks.astype(jnp.float32), later_states, precision=highest
        )
        + later_norms[:, None, :, :]
    )
    grad_values = jnp.einsum(
        "nhst,nshv->nthv", kernel_low, grad_numerator, preferred_element_type=jnp.float32
    ) + jnp.einsum("nthf,nhfv->nthv", phi_key.astype(jnp.float32), later_states, precision=highest)
    grad_values_low = grad_values.reshape(row_count, HEADS * VDIM).astype(jnp.bfloat16)
    grad_queries = jnp.einsum(
        "nhst,nthf->nshf", grad_scores, key_blocks, preferred_element_type=jnp.float32
    ) * 0.25 + 0.5 * features_back(query_scaled, grad_phi_query)
    grad_queries_low = grad_queries.reshape(row_count, HEADS * FDIM).astype(jnp.bfloat16)
    grad_keys = jnp.einsum(
        "nhst,nshf->nthf", grad_scores, query_blocks, preferred_element_type=jnp.float32
    ) * 0.25 + 0.5 * features_back(key_scaled, grad_phi_key)
    grad_keys_low = grad_keys.reshape(row_count, HEADS * FDIM).astype(jnp.bfloat16)
    grad_query_full = jnp.einsum(
        "td,tk->dk", normed_one_low, grad_queries_low, preferred_element_type=jnp.float32
    )
    grad_key_full = jnp.einsum(
        "td,tk->dk", normed_one_low, grad_keys_low, preferred_element_type=jnp.float32
    )
    grad_value_full = jnp.einsum(
        "td,tk->dk", normed_one_low, grad_values_low, preferred_element_type=jnp.float32
    )
    grad_normed_one = (
        jnp.einsum("tk,dk->td", grad_queries_low, query_full, preferred_element_type=jnp.float32)
        + jnp.einsum("tk,dk->td", grad_keys_low, key_full, preferred_element_type=jnp.float32)
        + jnp.einsum("tk,dk->td", grad_values_low, value_full, preferred_element_type=jnp.float32)
    )
    grad_from_norm, grad_gain_one = norm_backward(
        residual, inv_rms_one, norm_one_gain, grad_normed_one
    )
    grad_tokens = (grad_middle + grad_from_norm)[None]
    shards = (
        lax.psum_scatter(
            grad_gain_one.astype(jnp.bfloat16), "fsdp", scatter_dimension=0, tiled=True
        ).astype(jnp.float32),
        lax.psum_scatter(
            grad_query_full.astype(jnp.bfloat16), "fsdp", scatter_dimension=0, tiled=True
        ).astype(jnp.float32),
        lax.psum_scatter(
            grad_key_full.astype(jnp.bfloat16), "fsdp", scatter_dimension=0, tiled=True
        ).astype(jnp.float32),
        lax.psum_scatter(
            grad_value_full.astype(jnp.bfloat16), "fsdp", scatter_dimension=0, tiled=True
        ).astype(jnp.float32),
        lax.psum_scatter(
            grad_out_proj.astype(jnp.bfloat16), "fsdp", scatter_dimension=0, tiled=True
        ).astype(jnp.float32),
        lax.psum_scatter(
            grad_gain_two.astype(jnp.bfloat16), "fsdp", scatter_dimension=0, tiled=True
        ).astype(jnp.float32),
        lax.psum_scatter(
            grad_gate_full.astype(jnp.bfloat16), "fsdp", scatter_dimension=0, tiled=True
        ).astype(jnp.float32),
        lax.psum_scatter(
            grad_up_full.astype(jnp.bfloat16), "fsdp", scatter_dimension=0, tiled=True
        ).astype(jnp.float32),
        lax.psum_scatter(
            grad_down_full.astype(jnp.bfloat16), "fsdp", scatter_dimension=0, tiled=True
        ).astype(jnp.float32),
    )
    totals = lax.psum(
        (
            shards[0],
            shards[1],
            shards[2],
            shards[3],
            shards[4],
            shards[5],
            shards[6],
            shards[7],
            shards[8],
        ),
        "ctx",
    )
    return (
        output,
        grad_tokens,
        totals[0],
        totals[1],
        totals[2],
        totals[3],
        totals[4],
        totals[5],
        totals[6],
        totals[7],
        totals[8],
    )


def solution(mesh):
    in_specs = (
        P("fsdp", "ctx", None),
        P("fsdp", None),
        P("fsdp"),
        P("fsdp", None),
        P("fsdp", None),
        P("fsdp", None),
        P("fsdp", None),
        P("fsdp"),
        P("fsdp", None),
        P("fsdp", None),
        P("fsdp", None),
        P("fsdp", "ctx", None),
    )
    out_specs = (
        P("fsdp", "ctx", None),
        P("fsdp", "ctx", None),
        P("fsdp"),
        P("fsdp", None),
        P("fsdp", None),
        P("fsdp", None),
        P("fsdp", None),
        P("fsdp"),
        P("fsdp", None),
        P("fsdp", None),
        P("fsdp", None),
    )
    return jax.shard_map(body, mesh=mesh, in_specs=in_specs, out_specs=out_specs, check_vma=False)
```

profile of v0, /device:TPU:0, one launch (start us, length us, event | category | flops | bytes accessed | tf_op | source)
XLA Modules:
  0.0 1292.5 jit_solution(17293718670228395038)
XLA Ops:
  8.6 6.0 all-gather
  16.1 9.3 all_gather.45
  28.8 7.1 all-gather.12.cloned.1.call-done
  42.4 7.3 all_gather.44
  81.6 7.7 all-gather.14.cloned.1.call-done
  96.9 118.5 %all-gather.16.cloned.1.call-done = bf16[4096,1024]{1,0:T(8,128)(2,1)} async-done(((bf16[512,1024]{1,0:T(8,128)(2,1)}), bf16[4096,1024]{1,0:T(8,128)(2,1)}) %all-gather.16.cloned.1.call-update) | async-done | bytes 8388624 | tf_op jit(solution)/shard_map/all_gather | solution.py:119
  215.5 22.2 %reshape.269 = bf16[2,8,256,16,64]{4,3,2,1,0:T(8,128)(2,1)} reshape(bf16[4096,1024]{1,0:T(8,128)(2,1)} %all-gather.16.cloned.1.call-done) | data formatting | bytes 16777216 | tf_op jit(solution)/shard_map/reshape | solution.py:124
  237.7 19.7 %copy.112 = bf16[2,8,256,16,64]{2,4,3,1,0:T(8,128)(2,1)} copy(bf16[2,8,256,16,64]{4,3,2,1,0:T(8,128)(2,1)} %reshape.269) | data formatting | bytes 16777216
  257.4 111.2 %while.26 = (s32[]{:T(128)}, f32[2,16,273,64]{2,0,3,1:T(2,128)S(1)}, f32[2,16,273]{2,0,1:T(2,128)S(1)}, s32[2,8]{1,0:T(2,128)S(1)}, s32[2]{0:T(128)S(1)}, /*inde...) while((s32[]{:T(128)}, ...), condition=%wide.region_3.4_spmd.clone, body=%wide.region_1.3_spmd.clone.sunk | while | flops 1343690752 | bytes 159030480 | solution.py:143
  264.4 5.8 copy-done
  270.2 8.2 convert_reduce_fusion.2
  278.4 13.8 %fusion.184 = f32[8,16,273,64]{2,3,1,0:T(8,128)} fusion(bf16[8,256,16,256]{1,3,2,0:T(8,128)(2,1)} %bitcast.288, bf16[8,256,16,16]{1,3,2,0:T(8,128)(2,1)} %copy-done.1, bf16[273]{0:T(512)(128)(2,1)S(1)} %pad.clone.2, bf16[2,8,256,16,64]{2,4,3,1,0:T(8,128)(2,1)} %get-tuple-element.396, s32[]{:T(128)S(6)} %copy.272), kind=kOutput, calls=%fused_computation.5.clone.1 | convolution fusion | flops 1198718976 | bytes 30966310 | tf_op jit(solution)/shard_map/while/body/eval_jaxpr/gthf,gthv->ghfv/dot_general | solution.py:130
  292.3 19.9 %select_add_fusion.4 = f32[2,16,273,64]{2,0,3,1:T(2,128)S(1)} fusion(f32[2,16,273,64]{2,0,3,1:T(2,128)S(1)} %get-tuple-element.380, pred[]{:T(512)S(6)} %compare.6, f32[8,16,273,64]{2,3,1,0:T(8,128)} %fusion.184, s32[8]{0:T(128)S(1)} %fusion.185, s32[2]{0:T(128)S(1)} %get-tuple-element.394), kind=kOutput, calls=%fused_computation.9.clone.1 | convolution fusion | flops 54792208 | bytes 13418537 | tf_op jit(solution)/shard_map/while/body/eval_jaxpr/ig,ghfv->ihfv/dot_general | solution.py:137
  319.4 5.8 copy-done
  325.2 8.2 convert_reduce_fusion.2
  333.4 15.2 %fusion.184 = f32[8,16,273,64]{2,3,1,0:T(8,128)} fusion(bf16[8,256,16,256]{1,3,2,0:T(8,128)(2,1)} %bitcast.288, bf16[8,256,16,16]{1,3,2,0:T(8,128)(2,1)} %copy-done.1, bf16[273]{0:T(512)(128)(2,1)S(1)} %pad.clone.2, bf16[2,8,256,16,64]{2,4,3,1,0:T(8,128)(2,1)} %get-tuple-element.396, s32[]{:T(128)S(6)} %copy.272), kind=kOutput, calls=%fused_computation.5.clone.1 | convolution fusion | flops 1198718976 | bytes 30966310 | tf_op jit(solution)/shard_map/while/body/eval_jaxpr/gthf,gthv->ghfv/dot_general | solution.py:130
  348.6 19.3 %select_add_fusion.4 = f32[2,16,273,64]{2,0,3,1:T(2,128)S(1)} fusion(f32[2,16,273,64]{2,0,3,1:T(2,128)S(1)} %get-tuple-element.380, pred[]{:T(512)S(6)} %compare.6, f32[8,16,273,64]{2,3,1,0:T(8,128)} %fusion.184, s32[8]{0:T(128)S(1)} %fusion.185, s32[2]{0:T(128)S(1)} %get-tuple-element.394), kind=kOutput, calls=%fused_computation.9.clone.1 | convolution fusion | flops 54792208 | bytes 13418537 | tf_op jit(solution)/shard_map/while/body/eval_jaxpr/ig,ghfv->ihfv/dot_general | solution.py:137
  389.7 8.5 fusion.122
  398.3 8.7 fusion.121
  407.0 12.3 multiply_convert_fusion.5
  427.1 6.2 fusion.123
  433.4 6.2 multiply_reduce_fusion
  457.8 6.4 bitcast_add_fusion
  470.3 16.5 %fusion.44 = f32[2,256,16,16]{1,3,2,0:T(8,128)S(1)} fusion(f32[2,256,16,16,16]{1,4,3,2,0:T(8,128)} %bitcast.293, f32[2,256,16,16]{1,3,2,0:T(8,128)S(1)} %copy-done.21), kind=kLoop, calls=%fused_computation.67 | loop fusion | flops 6160384 | bytes 9437184 | tf_op jit(solution)/shard_map/...ab,...b->...a/dot_general | solution.py:32
  486.8 5.7 multiply_convert_fusion.3
  502.1 7.6 convolution_convert_fusion.2
  511.5 6.2 convolution_convert_fusion
  530.6 31.4 %all_gather.55 = bf16[4096,16]{0,1:T(8,128)(2,1)S(1)} all-gather(bf16[512,16]{0,1:T(8,128)(2,1)S(1)} %bitcast.321), channel_id=1, replica_groups=mesh['ctx'=8,'fsdp'=4] {'ctx'}, dimensions={0}, use_global_device_ids=true | all-gather | bytes 147456 | tf_op jit(solution)/shard_map/all_gather | solution.py:220
  569.9 22.2 %reshape.271 = bf16[2,8,256,16,64]{4,3,2,1,0:T(8,128)(2,1)} reshape(bf16[4096,1024]{1,0:T(8,128)(2,1)} %all-gather.28.cloned.1.call-done) | data formatting | bytes 16777216 | tf_op jit(solution)/shard_map/reshape | solution.py:225
  592.1 19.7 %copy.135 = bf16[2,8,256,16,64]{2,4,3,1,0:T(8,128)(2,1)} copy(bf16[2,8,256,16,64]{4,3,2,1,0:T(8,128)(2,1)} %reshape.271) | data formatting | bytes 16777216
  611.7 114.5 %while.27 = (s32[]{:T(128)}, f32[2,16,273,64]{2,0,3,1:T(2,128)S(1)}, f32[2,16,273]{2,0,1:T(2,128)S(1)}, s32[2,8]{1,0:T(2,128)S(1)}, s32[2]{0:T(128)S(1)}, /*inde...) while((s32[]{:T(128)}, ...), condition=%wide.region_9.10_spmd.clone, body=%wide.region_8.9_spmd.clone.sunk | while | flops 1352671360 | bytes 92249264 | solution.py:248
  614.5 8.8 multiply_convert_fusion.12
  623.3 9.2 fusion.193
  632.5 16.2 %fusion.191 = f32[8,16,273,64]{2,3,1,0:T(8,128)} fusion(bf16[8,256,16,256]{1,3,2,0:T(8,128)(2,1)} %bitcast.290, bf16[8,256,16,16]{1,3,2,0:T(8,128)(2,1)} %copy-done.9, bf16[273]{0:T(512)(128)(2,1)S(1)} %pad.3.clone.2, bf16[2,8,256,16,64]{2,4,3,1,0:T(8,128)(2,1)} %get-tuple-element.431, s32[]{:T(128)S(6)} %copy.281), kind=kOutput, calls=%fused_computation.30.clone.1 | convolution fusion | flops 1198718976 | bytes 30966310 | tf_op jit(solution)/shard_map/while/body/eval_jaxpr/gthf,gthv->ghfv/dot_general | solution.py:232
  648.8 19.8 %select_add_fusion.5 = f32[2,16,273,64]{2,0,3,1:T(2,128)S(1)} fusion(f32[2,16,273,64]{2,0,3,1:T(2,128)S(1)} %get-tuple-element.414, pred[]{:T(512)S(6)} %compare.7, f32[8,16,273,64]{2,3,1,0:T(8,128)} %fusion.191, s32[8]{0:T(128)S(1)} %fusion.192, s32[2]{0:T(128)S(1)} %get-tuple-element.429), kind=kOutput, calls=%fused_computation.35.clone.1 | convolution fusion | flops 54792208 | bytes 13418537 | tf_op jit(solution)/shard_map/while/body/eval_jaxpr/ig,ghfv->ihfv/dot_general | solution.py:242
  671.6 8.8 multiply_convert_fusion.12
  680.4 9.3 fusion.193
  689.7 16.1 %fusion.191 = f32[8,16,273,64]{2,3,1,0:T(8,128)} fusion(bf16[8,256,16,256]{1,3,2,0:T(8,128)(2,1)} %bitcast.290, bf16[8,256,16,16]{1,3,2,0:T(8,128)(2,1)} %copy-done.9, bf16[273]{0:T(512)(128)(2,1)S(1)} %pad.3.clone.2, bf16[2,8,256,16,64]{2,4,3,1,0:T(8,128)(2,1)} %get-tuple-element.431, s32[]{:T(128)S(6)} %copy.281), kind=kOutput, calls=%fused_computation.30.clone.1 | convolution fusion | flops 1198718976 | bytes 30966310 | tf_op jit(solution)/shard_map/while/body/eval_jaxpr/gthf,gthv->ghfv/dot_general | solution.py:232
  705.7 19.7 %select_add_fusion.5 = f32[2,16,273,64]{2,0,3,1:T(2,128)S(1)} fusion(f32[2,16,273,64]{2,0,3,1:T(2,128)S(1)} %get-tuple-element.414, pred[]{:T(512)S(6)} %compare.7, f32[8,16,273,64]{2,3,1,0:T(8,128)} %fusion.191, s32[8]{0:T(128)S(1)} %fusion.192, s32[2]{0:T(128)S(1)} %get-tuple-element.429), kind=kOutput, calls=%fused_computation.35.clone.1 | convolution fusion | flops 54792208 | bytes 13418537 | tf_op jit(solution)/shard_map/while/body/eval_jaxpr/ig,ghfv->ihfv/dot_general | solution.py:242
  726.2 6.9 add_bitcast_fusion
  739.2 17.3 %fusion.41 = f32[2,256,16,16]{1,3,2,0:T(8,128)} fusion(f32[2,256,16,16,16]{1,4,3,2,0:T(8,128)} %bitcast.294, f32[2,256,16,16]{1,3,2,0:T(8,128)S(1)} %copy-done.23), kind=kLoop, calls=%fused_computation.63 | loop fusion | flops 6160384 | bytes 9437184 | tf_op jit(solution)/shard_map/...ab,...b->...a/dot_general | solution.py:32
  761.8 8.4 fusion.48
  770.3 6.2 fusion.81
  785.7 7.7 fusion.80
  803.5 5.9 all-reduce.3
  813.0 7.9 reduce-scatter.10.cloned.1.call-done
  820.9 34.4 %reduce-scatter.12.cloned.1.call-done = bf16[256,1024]{1,0:T(8,128)(2,1)} async-done(((bf16[1024,1024]{1,0:T(8,128)(2,1)}), bf16[256,1024]{1,0:T(8,128)(2,1)}) %reduce-scatter.12.cloned.1.call-update) | async-done | bytes 524304 | tf_op jit(solution)/shard_map/reduce_scatter | solution.py:302
  855.3 430.5 %all-reduce.5 = (f32[256]{0:T(256)}, f32[256,256]{1,0:T(8,128)}, f32[256,256]{1,0:T(8,128)}, f32[256,1024]{1,0:T(8,128)}, f32[256,1024]{1,0:T(8,128)}, /*index=5...) all-reduce(f32[256]{0:T(256)S(1)} %get-tuple-element.267, ...), channel_id=1, replica_groups=mesh['ctx'=8,'fsdp'=4] {'ctx'}, use_global_device_ids=true, to_apply=%region_13.14 | all-reduce | flops 2769408 | bytes 16617472 | tf_op jit(solution)/shard_map/psum | solution.py:321
  (302 shorter events, 190.8 us)
Async XLA Ops:
  7.2 28.8 %copy-start.11 = (bf16[1,512,1024]{2,1,0:T(8,128)(2,1)S(1)}, bf16[1,512,1024]{2,1,0:T(8,128)(2,1)}, u32[]{:S(2)}) copy-start(bf16[1,512,1024]{2,1,0:T(8,128)(2,1)} %param.16) | copy-start | bytes 3145732
  7.2 28.7 %all-gather.12.cloned.1.call-start = ((), (), s32[]{:S(2)}) async-start(), calls=%async_computation.7 | async-start | bytes 2621440 | tf_op jit(solution)/shard_map/all_gather | solution.py:73
  7.9 81.4 %all-gather.14.cloned.1.call-start = ((), (), s32[]{:S(2)}) async-start(), calls=%async_computation.8 | async-start | bytes 2359296 | tf_op jit(solution)/shard_map/all_gather | solution.py:118
  14.6 35.1 %copy-start.53 = (f32[4,1,256]{2,1,0:T(1,128)}, f32[4,1,256]{2,1,0:T(1,128)S(1)}, u32[]{:S(2)}) copy-start(f32[4,1,256]{2,1,0:T(1,128)S(1)} %convert_element_type.281) | copy-start | bytes 12292
  26.1 23.6 %copy-start.58 = (f32[512]{0:T(512)}, f32[512]{0:T(512)S(1)}, u32[]{:S(2)}) copy-start(f32[512]{0:T(512)S(1)} %get-tuple-element.253) | copy-start | bytes 6148
  28.7 186.7 %all-gather.16.cloned.1.call-start = ((), (), s32[]{:S(2)}) async-start(), calls=%async_computation.9 | async-start | bytes 9437184 | tf_op jit(solution)/shard_map/all_gather | solution.py:119
  39.8 343.9 %all-gather.18.cloned.1.call-start = ((), (), s32[]{:S(2)}) async-start(), calls=%async_computation.10 | async-start | bytes 2621440 | tf_op jit(solution)/shard_map/all_gather | solution.py:74
  40.4 13.2 %copy-start.39 = (bf16[512,256]{1,0:T(8,128)(2,1)S(1)}, bf16[512,256]{1,0:T(8,128)(2,1)}, u32[]{:S(2)}) copy-start(bf16[512,256]{1,0:T(8,128)(2,1)} %convolution_convert_fusion.8) | copy-start | bytes 786436
  40.4 349.3 %all-gather.22.cloned.1.call-start = ((), (), s32[]{:S(2)}) async-start(), calls=%async_computation.12 | async-start | bytes 7045120 | tf_op jit(solution)/shard_map/all_gather | solution.py:77
  41.0 13.4 %copy-start.66 = (s32[1,16]{1,0:T(1,128)S(1)}, s32[1,16]{1,0:T(1,128)}, u32[]{:S(2)}) copy-start(s32[1,16]{1,0:T(1,128)} %param.17) | copy-start | bytes 196
  41.0 14.7 %copy-start.67 = (bf16[256]{0:T(256)(128)(2,1)S(1)}, bf16[256]{0:T(256)(128)(2,1)}, u32[]{:S(2)}) copy-start(bf16[256]{0:T(256)(128)(2,1)} %param.23) | copy-start | bytes 1540
  41.0 357.3 %all-gather.20.cloned.1.call-start = ((), (), s32[]{:S(2)}) async-start(), calls=%async_computation.11 | async-start | bytes 7045120 | tf_op jit(solution)/shard_map/all_gather | solution.py:76
  41.6 365.4 %all-gather.24.cloned.1.call-start = ((), (), s32[]{:S(2)}) async-start(), calls=%async_computation.13 | async-start | bytes 7045120 | tf_op jit(solution)/shard_map/all_gather | solution.py:78
  42.3 480.5 %all-gather.26.cloned.1.call-start = ((), (), s32[]{:S(2)}) async-start(), calls=%async_computation.14 | async-start | bytes 2359296 | tf_op jit(solution)/shard_map/all_gather | solution.py:218
  51.7 518.2 %all-gather.28.cloned.1.call-start = ((), (), s32[]{:S(2)}) async-start(), calls=%async_computation.15 | async-start | bytes 9437184 | tf_op jit(solution)/shard_map/all_gather | solution.py:219
  62.4 11.1 copy-start.28
  65.0 8.5 copy-start.20
  257.3 111.2 %copy-start.64 = (bf16[273]{0:T(512)(128)(2,1)S(1)}, bf16[273]{0:T(512)(128)(2,1)}, u32[]{:S(2)}) copy-start(bf16[273]{0:T(512)(128)(2,1)} %pad.9.clone) | copy-start | bytes 1642
  368.6 9.7 slice-start
  387.8 10.4 copy-start.56
  427.1 6.2 copy-start.24
  427.1 6.2 copy-start.51
  427.1 6.3 copy-start.57
  433.3 6.3 copy-start.36
  433.3 6.3 copy-start.62
  444.8 348.6 %reduce-scatter.8.cloned.1.call-start = ((), (), s32[]{:S(2)}) async-start(), calls=%async_computation.16 | async-start | bytes 655360 | tf_op jit(solution)/shard_map/reduce_scatter | solution.py:296
  457.1 29.7 %copy-start.10 = (bf16[2,256,16,64]{1,3,2,0:T(8,128)(2,1)}, bf16[2,256,16,64]{1,3,2,0:T(8,128)(2,1)S(1)}, u32[]{:S(2)}) copy-start(bf16[2,256,16,64]{1,3,2,0:T(8,128)(2,1)S(1)} %get-tuple-element.246) | copy-start | bytes 3145732
  470.3 16.5 %copy-start.16 = (bf16[2,256,16,64]{1,3,2,0:T(8,128)(2,1)S(1)}, bf16[2,256,16,64]{1,3,2,0:T(8,128)(2,1)}, u32[]{:S(2)}) copy-start(bf16[2,256,16,64]{1,3,2,0:T(8,128)(2,1)} %copy.107) | copy-start | bytes 3145732
  486.8 7.8 copy-start.31
  499.4 294.0 %reduce-scatter.14.cloned.1.call-start = ((), (), s32[]{:S(2)}) async-start(), calls=%async_computation.19 | async-start | bytes 2621440 | tf_op jit(solution)/shard_map/reduce_scatter | solution.py:305
  502.1 291.3 %reduce-scatter.20.cloned.1.call-start = ((), (), s32[]{:S(2)}) async-start(), calls=%async_computation.22 | async-start | bytes 7045120 | tf_op jit(solution)/shard_map/reduce_scatter | solution.py:317
  509.7 283.7 %reduce-scatter.18.cloned.1.call-start = ((), (), s32[]{:S(2)}) async-start(), calls=%async_computation.21 | async-start | bytes 7045120 | tf_op jit(solution)/shard_map/reduce_scatter | solution.py:314
  517.7 278.4 %reduce-scatter.16.cloned.1.call-start = ((), (), s32[]{:S(2)}) async-start(), calls=%async_computation.20 | async-start | bytes 7045120 | tf_op jit(solution)/shard_map/reduce_scatter | solution.py:311
  522.8 7.8 copy-start.52
  526.9 35.8 %copy-start.37 = (bf16[512,1024]{1,0:T(8,128)(2,1)S(1)}, bf16[512,1024]{1,0:T(8,128)(2,1)}, u32[]{:S(2)}) copy-start(bf16[512,1024]{1,0:T(8,128)(2,1)} %multiply_convert_fusion.8) | copy-start | bytes 3145732
  526.9 35.8 %copy-start.71 = (bf16[512,2752]{0,1:T(8,128)(2,1)S(1)}, bf16[512,2752]{0,1:T(8,128)(2,1)}, u32[]{:S(2)}) copy-start(bf16[512,2752]{0,1:T(8,128)(2,1)} %get-tuple-element.244) | copy-start | bytes 8454148
  567.6 253.3 %reduce-scatter.10.cloned.1.call-start = ((), (), s32[]{:S(2)}) async-start(), calls=%async_computation.17 | async-start | bytes 655360 | tf_op jit(solution)/shard_map/reduce_scatter | solution.py:299
  592.0 19.7 %copy-start.46 = (s32[2]{0:T(128)S(1)}, s32[2]{0:T(128)}, u32[]{:S(2)}) copy-start(s32[2]{0:T(128)} %copy-done.45) | copy-start | bytes 28
  592.0 19.7 %copy-start.69 = (s32[2,8]{1,0:T(2,128)S(1)}, s32[2,8]{1,0:T(2,128)}, u32[]{:S(2)}) copy-start(s32[2,8]{1,0:T(2,128)} %copy-done.68) | copy-start | bytes 196
  614.5 8.8 copy-start.9
  671.6 8.8 copy-start.9
  739.2 17.3 %copy-start.3 = (bf16[2,16,256,256]{2,3,1,0:T(8,128)(2,1)S(1)}, bf16[2,16,256,256]{2,3,1,0:T(8,128)(2,1)}, u32[]{:S(2)}) copy-start(bf16[2,16,256,256]{2,3,1,0:T(8,128)(2,1)} %copy-done.2) | copy-start | bytes 12582916
  739.2 17.3 %copy-start.29 = (bf16[2,256,16,16]{1,0,3,2:T(2,128)(2,1)S(1)}, bf16[2,256,16,16]{1,0,3,2:T(2,128)(2,1)}, u32[]{:S(2)}) copy-start(bf16[2,256,16,16]{1,0,3,2:T(2,128)(2,1)} %copy-done.28) | copy-start | bytes 786436
  770.2 85.1 %reduce-scatter.12.cloned.1.call-start = ((), (), s32[]{:S(2)}) async-start(), calls=%async_computation.18 | async-start | bytes 2621440 | tf_op jit(solution)/shard_map/reduce_scatter | solution.py:302
  778.8 6.9 copy-start.8
  799.3 10.2 copy-start.19
  799.4 10.2 copy-start.61
  803.5 51.8 %copy-start.48 = (bf16[256,256]{1,0:T(8,128)(2,1)S(1)}, bf16[256,256]{1,0:T(8,128)(2,1)}, u32[]{:S(2)}) copy-start(bf16[256,256]{1,0:T(8,128)(2,1)} %reduce-scatter.8.cloned.1.call-done) | copy-start | bytes 393220
  (45 other events, 174.0 us)
Sparse Core Ops, SparseCore 0:
  9.6 26.2 all-gather.11
  38.6 50.6 all-gather.13
  92.0 123.4 all-gather.15
  216.9 20.7 all-gather.17
  239.1 43.3 all-gather.21
  283.9 43.3 all-gather.19
  328.9 42.6 all-gather.23
  373.7 49.2 all-gather.25
  444.9 124.8 all-gather.27
  572.2 20.0 reduce-scatter.7
  594.9 31.4 reduce-scatter.13
  628.8 54.0 reduce-scatter.19
  685.6 53.9 reduce-scatter.17
  742.1 54.0 reduce-scatter.15
  799.2 21.6 reduce-scatter.9
  823.8 31.4 reduce-scatter.11
where the time goes:
time: 1300 us; the launch traced here: 1290 us
  blocking collectives  495 us (38%)
  matrix products  317 us (24%)
  waiting for transfers between devices  184 us (14%)
  local copies, waits for them, and re-layouts  168 us (13%)
  other arithmetic  111 us (9%)
  between operations  15.6 us (1%)
    psum x1, blocking collectives, body(): lax.psum((shards[0], shards[1], shards[2], shards[3], shards[4], shards[5...  430 us
    all_gather x1, waiting for transfers between devices, body(): value_piece = lax.all_gather(values_all, 'ctx', axis=0, tiled=True)  119 us
    unnamed x156, local copies, waits for them, and re-layouts  63.5 us
    dot_general x2, matrix products, one_group(): jnp.einsum('ig,ghfv->ihfv', later_mask, grad_states, precision=highest)  39.6 us
    dot_general x2, matrix products, one_group(): jnp.einsum('ig,ghfv->ihfv', earlier, states, precision=highest)  39.2 us
    another operation x12, other arithmetic  37.8 us
    reduce_scatter x1, waiting for transfers between devices, body(): lax.psum_scatter(grad_value_full.astype(jnp.bfloat16), 'fsdp', scatter_di...  34.4 us
    dot_general x2, other arithmetic, features_back(): jnp.einsum('...ab,...b->...a', square + jnp.swapaxes(square, -1, -2), sca...  33.7 us
  transfers between devices with their start and end apart: 16, of which 7 were waited for; matrix products, arithmetic and copies ran while one was open for 44% of the time, Pallas kernels for 0%

commit v1 on v0

v1 whole, which is shorter than its diff:
```python
import jax
import jax.numpy as jnp
from jax import lax
from jax.experimental import pallas as pl
from jax.experimental.pallas import tpu as pltpu
from jax.sharding import PartitionSpec as P

HEADS = 16
FDIM = 16
VDIM = 64
BLOCK = 256
GROUP = 8
FEAT = 160
STATE = GROUP // 2 * FEAT + 2 * GROUP
EPS = 1e-05
ROOT_HALF = 0.7071067811865476

f32 = jnp.float32
bf16 = jnp.bfloat16


def dims(lhs, rhs):
    return (((lhs,), (rhs,)), ((), ()))


def dot(lhs, rhs, contract):
    return lax.dot_general(lhs, rhs, dims(*contract), preferred_element_type=f32)


def turned(u, shift):
    return pltpu.roll(u, FDIM - shift, 0)


def features(u, pair_weight):
    rows = [u, u * u * ROOT_HALF]
    for shift in range(1, 8):
        rows.append(u * turned(u, shift) * ROOT_HALF)
    rows.append(u[:8] * u[8:] * ROOT_HALF)
    one = (lax.broadcasted_iota(jnp.int32, (8, u.shape[1]), 0) == 0).astype(f32)
    linear = jnp.concatenate(rows[:2], axis=0).astype(bf16)
    pairs = jnp.concatenate(rows[2:], axis=0).astype(bf16) * pair_weight
    del rows
    return jnp.concatenate([linear.astype(f32), pairs.astype(f32), one], axis=0).astype(bf16)


def features_back(u, g):
    total = g[:16] + (2.0 * ROOT_HALF) * (g[16:32] * u)
    for shift in range(1, 8):
        here = (2.0 * ROOT_HALF) * g[16 + 16 * shift : 32 + 16 * shift]
        total = total + here * turned(u, shift) + pltpu.roll(here * u, shift, 0)
    here = (2.0 * ROOT_HALF) * g[144:152]
    return total + jnp.concatenate([here * u[8:], here * u[:8]], axis=0)


def halved(ref, head):
    return ref[head * FDIM : (head + 1) * FDIM, :].astype(f32) * 0.5


def write_states(out_ref, feat, value_pair, weight_row, head):
    pair = head // 2
    product = dot(feat, value_pair, (1, 1))
    half = slice(0, 64) if head % 2 == 0 else slice(64, 128)
    out_ref[0, 0, pair * FEAT : (pair + 1) * FEAT, half] = product[:, half].astype(bf16)
    norm = dot(weight_row, feat, (1, 1))
    base = GROUP // 2 * FEAT + 2 * head
    out_ref[0, 0, base : base + 1, :] = norm[:1, :128].astype(bf16)
    out_ref[0, 0, base + 1 : base + 2, :] = jnp.concatenate([norm[:1, 128:], jnp.zeros((1, 96), f32)], axis=1).astype(bf16)


def norm_row(state_ref, head):
    base = GROUP // 2 * FEAT + 2 * head
    return state_ref[0, 0, base : base + 1, :], state_ref[0, 0, base + 1 : base + 2, :32]


def head_state(state_ref, head):
    pair = head // 2
    return state_ref[0, 0, pair * FEAT : (pair + 1) * FEAT, 64 * (head % 2) : 64 * (head % 2) + 64]


def states_kernel(key_ref, value_ref, out_ref):
    ones = jnp.ones((8, BLOCK), bf16)
    for head in range(GROUP):
        feat = features(halved(key_ref, head), 1.0)
        pair = head // 2
        write_states(out_ref, feat, value_ref[pair * 128 : (pair + 1) * 128, :], ones, head)


def intra_kernel(query_ref, key_ref, value_ref, numer_ref, denom_ref):
    for head in range(GROUP):
        rows = slice(head * FDIM, (head + 1) * FDIM)
        wide = slice(head * VDIM, (head + 1) * VDIM)
        scores = dot(key_ref[rows, :], query_ref[rows, :], (0, 0)) * 0.25
        kernel = 1.0 + scores + 0.5 * scores * scores
        denom_ref[head : head + 1, :] = jnp.sum(kernel, axis=0, keepdims=True)
        numer_ref[wide, :] = dot(value_ref[wide, :], kernel.astype(bf16), (1, 0))


def inter_kernel(query_ref, prefix_ref, numer_ref, denom_in_ref, atten_ref, denom_ref):
    for head in range(GROUP):
        wide = slice(head * VDIM, (head + 1) * VDIM)
        feat = features(halved(query_ref, head), 2.0)
        numer = numer_ref[wide, :] + dot(head_state(prefix_ref, head), feat, (0, 0))
        first, second = norm_row(prefix_ref, head)
        denom = denom_in_ref[head : head + 1, :] + dot(first, feat[:128], (1, 0)) + dot(second, feat[128:], (1, 0))
        denom_ref[head : head + 1, :] = denom
        atten_ref[wide, :] = (numer / denom).astype(bf16)


def grad_states_kernel(query_ref, atten_ref, denom_ref, grad_ref, gnumer_ref, gdenom_ref, out_ref):
    for pair in range(GROUP // 2):
        for head in (2 * pair, 2 * pair + 1):
            wide = slice(head * VDIM, (head + 1) * VDIM)
            denom = denom_ref[head : head + 1, :]
            grad = grad_ref[wide, :]
            gnumer_ref[wide, :] = (grad / denom).astype(bf16)
            gdenom = -jnp.sum(grad * atten_ref[wide, :].astype(f32), axis=0, keepdims=True) / denom
            gdenom_ref[head : head + 1, :] = gdenom.astype(bf16).astype(f32)
        for head in (2 * pair, 2 * pair + 1):
            feat = features(halved(query_ref, head), 1.0)
            weights = jnp.broadcast_to(gdenom_ref[head : head + 1, :], (8, BLOCK)).astype(bf16)
            write_states(out_ref, feat, gnumer_ref[pair * 128 : (pair + 1) * 128, :], weights, head)


def intra_back_kernel(
    query_ref, key_ref, value_ref, gnumer_ref, gdenom_ref, prefix_ref, gquery_ref, gkey_ref, gvalue_ref
):
    for head in range(GROUP):
        rows = slice(head * FDIM, (head + 1) * FDIM)
        wide = slice(head * VDIM, (head + 1) * VDIM)
        query, key = query_ref[rows, :], key_ref[rows, :]
        gnumer = gnumer_ref[wide, :]
        gdenom = gdenom_ref[head : head + 1, :]
        scores = dot(key, query, (0, 0)) * 0.25
        kernel = (1.0 + scores + 0.5 * scores * scores).astype(bf16)
        gkernel = dot(value_ref[wide, :], gnumer, (0, 0)) + gdenom
        gscores = ((1.0 + scores) * gkernel).astype(bf16)
        gvalue_ref[wide, :] = dot(gnumer, kernel, (1, 1))
        gkey_ref[rows, :] = dot(query, gscores, (1, 1)) * 0.25
        first, second = norm_row(prefix_ref, head)
        gdenom_low = gdenom.astype(bf16)
        outer_prod = jnp.concatenate([dot(first, gdenom_low, (0, 0)), dot(second, gdenom_low, (0, 0))], axis=0)
        gfeat = dot(head_state(prefix_ref, head), gnumer, (1, 0)) + outer_prod
        gquery = dot(key, gscores, (1, 0)) * 0.25 + 0.5 * features_back(halved(query_ref, head), gfeat)
        gquery_ref[rows, :] = gquery.astype(bf16)


def inter_back_kernel(key_ref, value_ref, later_ref, gkey_in_ref, gvalue_in_ref, gkey_ref, gvalue_ref):
    ones = jnp.ones((1, BLOCK), bf16)
    for head in range(GROUP):
        rows = slice(head * FDIM, (head + 1) * FDIM)
        wide = slice(head * VDIM, (head + 1) * VDIM)
        u = halved(key_ref, head)
        state = head_state(later_ref, head)
        first, second = norm_row(later_ref, head)
        outer_prod = jnp.concatenate([dot(first, ones, (0, 0)), dot(second, ones, (0, 0))], axis=0)
        gfeat = dot(state, value_ref[wide, :], (1, 0)) + outer_prod
        gkey_ref[rows, :] = (gkey_in_ref[rows, :] + 0.5 * features_back(u, gfeat)).astype(bf16)
        feat = features(u, 2.0)
        gvalue_ref[wide, :] = (gvalue_in_ref[wide, :] + dot(state, feat, (0, 0))).astype(bf16)


def attention_call(kernel, ins, outs, tokens, flops):
    blocks = tokens // BLOCK
    groups = HEADS // GROUP
    forms = {
        "narrow": ((GROUP * FDIM, BLOCK), lambda b, g: (g, b), (HEADS * FDIM, tokens)),
        "wide": ((GROUP * VDIM, BLOCK), lambda b, g: (g, b), (HEADS * VDIM, tokens)),
        "head": ((GROUP, BLOCK), lambda b, g: (g, b), (HEADS, tokens)),
        "state": ((1, 1, STATE, 128), lambda b, g: (b, g, 0, 0), (blocks, groups, STATE, 128)),
    }

    def spec(name):
        return pl.BlockSpec(forms[name][0], forms[name][1])

    def call(*arrays):
        moved = sum(a.size * a.dtype.itemsize for a in arrays)
        return pl.pallas_call(
            kernel,
            out_shape=[jax.ShapeDtypeStruct(forms[name][2], dtype) for name, dtype in outs],
            grid=(blocks, groups),
            in_specs=[spec(name) for name in ins],
            out_specs=[spec(name) for name, _ in outs],
            compiler_params=pltpu.CompilerParams(vmem_limit_bytes=40 << 20),
            cost_estimate=pl.CostEstimate(flops=flops, bytes_accessed=2 * moved, transcendentals=0),
        )(*arrays)

    return call


ORDER = (0, 2, 1, 3)


def place(step):
    return (step % 2) * 2 + step // 2


def ffn_kernel(me_ref, middle_ref, gain_ref, cot_ref, *refs):
    gates, ups, downs = refs[:4], refs[4:8], refs[8:12]
    output_ref, gmiddle_ref, branch_ref, ggain_ref = refs[12:16]
    gate_keep, gate_send, up_keep, up_send, down_keep, down_send = refs[16:22]
    normed, x_own, x_turned, cot_turned, down, total, gnormed = refs[22:]
    step = pl.program_id(0)
    me = me_ref[0]
    width = gates[0].shape[1]

    def columns(r):
        return pl.ds(pl.multiple_of((me ^ r) * width, width), width)

    def inverse():
        middle = middle_ref[...]
        return lax.rsqrt(jnp.mean(middle * middle, axis=-1, keepdims=True) + EPS)

    @pl.when(step == 0)
    def _():
        normed[...] = (middle_ref[...] * inverse() * gain_ref[...]).astype(bf16)
        for r in range(4):
            part = normed[:, columns(r)]
            x_own[:, r * width : (r + 1) * width] = part
            x_turned[r * width : (r + 1) * width, :] = part.T
        cot_turned[...] = cot_ref[...].T
        total[...] = jnp.zeros_like(total)
        gnormed[...] = jnp.zeros_like(gnormed)

    for at in range(4):

        @pl.when(step == at)
        def _(at=at):
            down[...] = downs[ORDER[at]][...]

    gate = dot(gates[0][...], x_turned[:width, :], (1, 0))
    up = dot(ups[0][...], x_turned[:width, :], (1, 0))
    for r in range(1, 4):
        x_part = x_turned[r * width : (r + 1) * width, :]
        gate = gate + dot(gates[r][...], x_part, (1, 0))
        up = up + dot(ups[r][...], x_part, (1, 0))
    ghidden = dot(down[...], cot_turned[...], (1, 0))
    sigmoid = jax.nn.sigmoid(gate)
    silu = gate * sigmoid
    hidden = (silu * up).astype(bf16)
    ggate = (ghidden * up * (sigmoid * (1.0 + gate * (1.0 - sigmoid)))).astype(bf16)
    gup = (ghidden * silu).astype(bf16)
    total[...] += dot(hidden, down[...], (0, 0))
    gdown = dot(hidden, cot_ref[...], (1, 0)).astype(bf16)

    @pl.when(step < 2)
    def _():
        down_keep[0] = gdown

    @pl.when(step >= 2)
    def _():
        down_send[0] = gdown

    for r in range(4):
        part = slice(r * width, (r + 1) * width)
        gnormed[:, part] += dot(ggate, gates[r][...], (0, 0)) + dot(gup, ups[r][...], (0, 0))
        x_part = x_own[:, part]
        (gate_send if r % 2 else gate_keep)[r // 2] = dot(ggate, x_part, (1, 0)).astype(bf16)
        (up_send if r % 2 else up_keep)[r // 2] = dot(gup, x_part, (1, 0)).astype(bf16)

    @pl.when(step == 3)
    def _():
        for r in range(4):
            gmiddle_ref[:, columns(r)] = gnormed[:, r * width : (r + 1) * width]
        middle, inv, cot = middle_ref[...], inverse(), cot_ref[...].astype(f32)
        grad = gmiddle_ref[...]
        output_ref[...] = (middle + total[...]).astype(bf16)
        ggain_ref[...] = jnp.broadcast_to(jnp.sum(grad * middle * inv, axis=0, keepdims=True), ggain_ref.shape)
        weighted = grad * gain_ref[...]
        slope = jnp.mean(weighted * middle, axis=-1, keepdims=True)
        gmiddle = cot + inv * weighted - middle * (inv * inv * inv) * slope
        gmiddle_ref[...] = gmiddle
        branch_ref[...] = gmiddle.astype(bf16)


def ffn_call(me, middle, gain, cot, gates, ups, downs):
    rows, model = middle.shape
    hidden, width = gates[0].shape
    tile = downs[0].shape[0]
    once = pl.Buffered(1)

    def whole(shape, **kw):
        return pl.BlockSpec(shape, lambda s, me: (0,) * len(shape), **kw)

    piece = pl.BlockSpec((tile, width), lambda s, me: (me[0] ^ place(s), 0))
    pair = pl.BlockSpec((2, tile, width), lambda s, me: (0, me[0] ^ place(s), 0))
    pair_shape = jax.ShapeDtypeStruct((2, hidden, width), bf16)
    down_shape = jax.ShapeDtypeStruct((2, tile, model), bf16)
    return pl.pallas_call(
        ffn_kernel,
        out_shape=[
            jax.ShapeDtypeStruct((rows, model), bf16),
            jax.ShapeDtypeStruct((rows, model), f32),
            jax.ShapeDtypeStruct((rows, model), bf16),
            jax.ShapeDtypeStruct((8, model), f32),
            pair_shape,
            pair_shape,
            pair_shape,
            pair_shape,
            down_shape,
            down_shape,
        ],
        grid_spec=pltpu.PrefetchScalarGridSpec(
            num_scalar_prefetch=1,
            grid=(4,),
            in_specs=[whole((rows, model), pipeline_mode=once), whole((1, model)), whole((rows, model), pipeline_mode=once)]
            + [piece] * 8
            + [whole((tile, model), pipeline_mode=once)] * 4,
            out_specs=[
                whole((rows, model), pipeline_mode=once),
                whole((rows, model), pipeline_mode=once),
                whole((rows, model), pipeline_mode=once),
                whole((8, model)),
                pair,
                pair,
                pair,
                pair,
                pl.BlockSpec((1, tile, model), lambda s, me: (jnp.minimum(s, 1), 0, 0)),
                pl.BlockSpec((1, tile, model), lambda s, me: (jnp.maximum(s - 2, 0), 0, 0)),
            ],
            scratch_shapes=[
                pltpu.VMEM((rows, model), bf16),
                pltpu.VMEM((rows, model), bf16),
                pltpu.VMEM((model, rows), bf16),
                pltpu.VMEM((model, rows), bf16),
                pltpu.VMEM((tile, model), bf16),
                pltpu.VMEM((rows, model), f32),
                pltpu.VMEM((rows, model), f32),
            ],
        ),
        compiler_params=pltpu.CompilerParams(vmem_limit_bytes=58 << 20),
        cost_estimate=pl.CostEstimate(
            flops=18 * rows * model * hidden, bytes_accessed=14 * hidden * model, transcendentals=0
        ),
    )(me, middle, gain, cot, *gates, *ups, *downs)


def out_grad_kernel(me_ref, atten_ref, branch_ref, keep_ref, send_ref):
    grad = dot(atten_ref[...], branch_ref[...], (1, 0)).astype(bf16)

    @pl.when(pl.program_id(0) < 2)
    def _():
        keep_ref[0] = grad

    @pl.when(pl.program_id(0) >= 2)
    def _():
        send_ref[0] = grad


def in_grad_kernel(me_ref, normed_ref, query_ref, key_ref, value_ref, gain_ref, keep_ref, send_ref):
    x = normed_ref[...].T
    parts = [dot(x, ref[...], (1, 1)) for ref in (query_ref, key_ref, value_ref)]
    grad = jnp.concatenate(parts + [gain_ref[...]], axis=1).astype(bf16)

    @pl.when(pl.program_id(0) < 2)
    def _():
        keep_ref[0] = grad

    @pl.when(pl.program_id(0) >= 2)
    def _():
        send_ref[0] = grad


def shard_grads(kernel, me, moving, moving_axis, fixed, also, width):
    size = moving.shape[moving_axis] // 4
    block = list(moving.shape)
    block[moving_axis] = size
    if moving_axis == 0:
        spec = pl.BlockSpec(tuple(block), lambda s, me: (me[0] ^ place(s), 0))
    else:
        spec = pl.BlockSpec(tuple(block), lambda s, me: (0, me[0] ^ place(s)))
    extra = [pl.BlockSpec((size, a.shape[1]), lambda s, me: (me[0] ^ place(s), 0)) for a in also]
    steady = [pl.BlockSpec(a.shape, lambda s, me: (0, 0)) for a in fixed]
    shape = jax.ShapeDtypeStruct((2, size, width), bf16)
    tokens = moving.shape[1 - moving_axis]
    return pl.pallas_call(
        kernel,
        out_shape=[shape, shape],
        grid_spec=pltpu.PrefetchScalarGridSpec(
            num_scalar_prefetch=1,
            grid=(4,),
            in_specs=[spec] + steady + extra,
            out_specs=[
                pl.BlockSpec((1, size, width), lambda s, me: (jnp.minimum(s, 1), 0, 0)),
                pl.BlockSpec((1, size, width), lambda s, me: (jnp.maximum(s - 2, 0), 0, 0)),
            ],
        ),
        compiler_params=pltpu.CompilerParams(vmem_limit_bytes=40 << 20),
        cost_estimate=pl.CostEstimate(
            flops=8 * tokens * size * width, bytes_accessed=16 * size * width, transcendentals=0
        ),
    )(me, moving, *fixed, *also)


CORE = [(0, 1), (1, 0), (2, 3), (3, 2)]
CHIP = [(0, 2), (2, 0), (1, 3), (3, 1)]


def pieces(shard, after=None):
    crossing = shard if after is None else lax.optimization_barrier((shard, after))[0]
    far = lax.ppermute(crossing, "fsdp", CHIP)
    return shard, lax.ppermute(shard, "fsdp", CORE), far, lax.ppermute(far, "fsdp", CORE)


def ordered(parts, place_bits):
    for bit in (1, 2):
        swap = (place_bits & bit) != 0
        parts = [jnp.where(swap, parts[j ^ bit], parts[j]) for j in range(4)]
    return parts


def summed(keep, send, own, count, axis):
    got = lax.ppermute(send, "fsdp", CORE)
    cross = (keep[1].astype(f32) + got[1].astype(f32)).astype(bf16)
    got_cross = lax.ppermute(cross, "fsdp", CHIP)
    total = keep[0].astype(f32) + got[0].astype(f32) + got_cross.astype(f32)
    if count != 8:
        return lax.psum(total.astype(bf16), "ctx").astype(f32)
    size = total.shape[axis]
    y, z = own % 2, own // 2

    def cut(array, index, parts):
        part = array.shape[axis] // parts
        return lax.dynamic_slice_in_dim(array, index * part, part, axis)

    def trade(array, bits):
        return lax.ppermute(array, "ctx", [(i, i ^ bits) for i in range(count)])

    got_half = trade(cut(total, 1 - y, 2).astype(bf16), 1)
    half = cut(total, y, 2) + got_half.astype(f32)
    mine = cut(half, z, 4)
    for k in (1, 2, 3):
        mine = mine + trade(cut(half, z ^ k, 4).astype(bf16), 2 * k).astype(f32)
    mine = mine.astype(bf16)
    near = [mine] + [trade(mine, 2 * k) for k in (1, 2, 3)]
    far = trade(jnp.concatenate(near, axis=axis), 1)
    far = [cut(far, k, 4) for k in range(4)]
    low = [jnp.where(y == 0, a, b) for a, b in zip(near, far)]
    high = [jnp.where(y == 0, b, a) for a, b in zip(near, far)]
    return jnp.concatenate(ordered(low, z) + ordered(high, z), axis=axis).astype(f32)


def masked_sums(pieces, masks, dtype):
    total = None
    for index, piece in enumerate(pieces):
        for block in range(piece.shape[0]):
            term = masks[:, index, block][:, None, None, None] * piece[block].astype(f32)[None]
            total = term if total is None else total + term
    return total.astype(dtype)


def exchange(own_states, positions, own, count, later):
    local = own_states.shape[0]
    table = positions.reshape(count, local)

    def mask(target, sources):
        there = table[target][:, None, None]
        here = table[jnp.stack(sources)][None]
        return ((here > there) if later else (here < there)).astype(f32)

    pieces, sources = [own_states], [own]
    for step in range(1, count // 2):
        pieces.append(lax.ppermute(pieces[-1], "ctx", [(i, (i + 2) % count) for i in range(count)]))
        sources.append((own - 2 * step) % count)
    partner = own ^ 1
    for_partner = masked_sums(pieces, mask(partner, sources), bf16)
    received = lax.ppermute(for_partner, "ctx", [(i, i ^ 1) for i in range(count)])
    return (masked_sums(pieces, mask(own, sources), f32) + received.astype(f32)).astype(bf16)


def body(count):
    def layer(
        tokens, block_pos, gain_attn, w_query, w_key, w_value, w_out, gain_ffn, w_gate, w_up, w_down, cotangent
    ):
        gather = lambda a: lax.all_gather(a, "fsdp", axis=0, tiled=True)
        own = lax.axis_index("ctx")
        me = lax.axis_index("fsdp").astype(jnp.int32).reshape(1)
        positions = block_pos[0]
        gains = gather(jnp.stack([gain_attn, gain_ffn], axis=1)).astype(f32)
        gain_one, gain_two = gains[:, 0], gains[:, 1]
        in_full = gather(jnp.concatenate([w_query, w_key, w_value], axis=1))
        gates = pieces(w_gate.T, in_full)
        ups = pieces(w_up.T, in_full)
        downs = pieces(w_down, gates[2])
        out_full = gather(w_out)
        residual = tokens[0].astype(f32)
        rows = residual.shape[0]
        inv_one = lax.rsqrt(jnp.mean(residual * residual, axis=-1, keepdims=True) + EPS)
        normed_one = (residual * inv_one * gain_one).astype(bf16)
        narrow = HEADS * FDIM
        projected = dot(in_full, normed_one, (0, 1)).astype(bf16)
        query, key, value = projected[:narrow], projected[narrow : 2 * narrow], projected[2 * narrow :]

        unit = 2 * rows * BLOCK * HEADS
        (own_states,) = attention_call(
            states_kernel, ("narrow", "wide"), (("state", bf16),), rows, unit * FEAT
        )(key, value)
        numer, denom = attention_call(
            intra_kernel, ("narrow", "narrow", "wide"), (("wide", f32), ("head", f32)), rows, unit * 256
        )(query, key, value)
        prefix = exchange(own_states, positions, own, count, False)
        atten, denom = attention_call(
            inter_kernel, ("narrow", "state", "wide", "head"), (("wide", bf16), ("head", f32)), rows, unit * FEAT
        )(query, prefix, numer, denom)

        middle = residual + dot(atten, out_full, (0, 0))
        results = ffn_call(me, middle, gain_two.reshape(1, -1), cotangent[0], gates, ups, downs)
        output, grad_middle, branch, grad_gain_two = results[:4]
        gate_keep, gate_send, up_keep, up_send, down_keep, down_send = results[4:]
        grad_atten = dot(out_full, branch, (1, 1))

        gnumer, gdenom, grad_states = attention_call(
            grad_states_kernel,
            ("narrow", "wide", "head", "wide"),
            (("wide", bf16), ("head", f32), ("state", bf16)),
            rows,
            unit * FEAT,
        )(query, atten, denom, grad_atten)
        gquery, gkey, gvalue = attention_call(
            intra_back_kernel,
            ("narrow", "narrow", "wide", "wide", "head", "state"),
            (("narrow", bf16), ("narrow", f32), ("wide", f32)),
            rows,
            unit * 512,
        )(query, key, value, gnumer, gdenom, prefix)
        later = exchange(grad_states, positions, own, count, True)
        gkey, gvalue = attention_call(
            inter_back_kernel,
            ("narrow", "wide", "state", "narrow", "wide"),
            (("narrow", bf16), ("wide", bf16)),
            rows,
            unit * 256,
        )(key, value, later, gkey, gvalue)
        gprojected = jnp.concatenate([gquery, gkey, gvalue], axis=0)
        gnormed_one = dot(gprojected, in_full, (0, 1))
        weighted_one = gnormed_one * gain_one
        grad_gain_one = jnp.sum(gnormed_one * residual * inv_one, axis=0)
        grad_tokens = (
            grad_middle
            + inv_one * weighted_one
            - residual * (inv_one * inv_one * inv_one) * jnp.mean(weighted_one * residual, axis=-1, keepdims=True)
        )[None]
        grad_gains = jnp.pad(jnp.stack([grad_gain_one, grad_gain_two[0]], axis=1), ((0, 0), (0, 126)))

        width = in_full.shape[1]
        out_keep, out_send = shard_grads(out_grad_kernel, me, atten, 0, [branch], [], branch.shape[1])
        in_keep, in_send = shard_grads(
            in_grad_kernel, me, normed_one, 1, [gquery, gkey, gvalue], [grad_gains], width + 128
        )
        down_grad = summed(down_keep, down_send, own, count, 1)
        gate_grad = summed(gate_keep, gate_send, own, count, 0).T
        up_grad = summed(up_keep, up_send, own, count, 0).T
        out_grad = summed(out_keep, out_send, own, count, 0)
        in_grad = summed(in_keep, in_send, own, count, 0)
        return (
            output[None],
            grad_tokens,
            in_grad[:, width],
            in_grad[:, :narrow],
            in_grad[:, narrow : 2 * narrow],
            in_grad[:, 2 * narrow : width],
            out_grad,
            in_grad[:, width + 1],
            gate_grad,
            up_grad,
            down_grad,
        )

    return layer


def solution(mesh):
    rows = P("fsdp", None)
    seqs = P("fsdp", "ctx", None)
    vec = P("fsdp")
    in_specs = (seqs, rows, vec, rows, rows, rows, rows, vec, rows, rows, rows, seqs)
    out_specs = (seqs, seqs, vec, rows, rows, rows, rows, vec, rows, rows, rows)
    return jax.shard_map(
        body(mesh.shape["ctx"]), mesh=mesh, in_specs=in_specs, out_specs=out_specs, check_vma=False
    )
```

time: 1300 us -> 601 us (0.46)
  blocking collectives: 495 us -> 5.98 us
  matrix products: 317 us -> 12.9 us
  local copies, waits for them, and re-layouts: 168 us -> 11.5 us
  waiting for transfers between devices: 184 us -> 340 us
  starting transfers between devices: 0.65 us -> 89.6 us
  Pallas kernels: 0 us -> 78.5 us
  other arithmetic: 111 us -> 39.4 us
    psum x1 -> x0, blocking collectives: 430 us -> none  [body(): lax.psum((shards[0], shards[1], shards[2], shards[3], shards[4], shards[5...]
    ppermute x0 -> x67, waiting for transfers between devices: none -> 314 us  [the longest x40 112 us: trade(): return lax.ppermute(array, 'ctx', [(i, i ^ bits) for i in range(count)])]
    dot_general x46 -> x4, matrix products: 317 us -> 12.9 us  [dot(): lax.dot_general(lhs, rhs, dims(*contract), preferred_element_type=f32)]
    all_gather x9 -> x2, waiting for transfers between devices: 136 us -> 25.3 us  [layer(): gather = lambda a: lax.all_gather(a, 'fsdp', axis=0, tiled=True)]
    ppermute x0 -> x67, starting transfers between devices: none -> 89.5 us  [the longest x40 77 us: trade(): return lax.ppermute(array, 'ctx', [(i, i ^ bits) for i in range(count)])]
    pallas_call x0 -> x9, Pallas kernels: none -> 78.5 us  [the longest x1 44.2 us: ffn_call(): pl.pallas_call(ffn_kernel, out_shape=[jax.ShapeDtypeStruct((rows, model),...]
    reshape x9 -> x0, local copies, waits for them, and re-layouts: 64.1 us -> none  [the longest x1 22.2 us: body(): value_piece.reshape(block_count // group_size, group_size, BLOCK, HEADS,...]
    unnamed x156 -> x81, local copies, waits for them, and re-layouts: 63.5 us -> 5.59 us
  transfers between devices with their start and end apart: 16 -> 69, of which waited for: 7 -> 32; matrix products, arithmetic and copies ran while one was open for 44% -> 8% of each run, Pallas kernels for 0% -> 5%
where the time goes in v1:
time: 601 us; the launch traced here: 593 us
  waiting for transfers between devices  340 us (57%)
  starting transfers between devices  89.6 us (15%)
  Pallas kernels  78.5 us (13%)
  other arithmetic  39.4 us (7%)
  between operations  15.4 us (3%)
  matrix products  12.9 us (2%)
  local copies, waits for them, and re-layouts  11.5 us (2%)
    ppermute x40, waiting for transfers between devices, trade(): return lax.ppermute(array, 'ctx', [(i, i ^ bits) for i in range(count)])  112 us
    ppermute x5, waiting for transfers between devices, summed(): got_cross = lax.ppermute(cross, 'fsdp', CHIP)  77.7 us
    ppermute x40, starting transfers between devices, trade(): return lax.ppermute(array, 'ctx', [(i, i ^ bits) for i in range(count)])  77 us
    ppermute x6, waiting for transfers between devices, exchange(): lax.ppermute(pieces[-1], 'ctx', [(i, (i + 2) % count) for i in range(coun...  57.9 us
    ppermute x3, waiting for transfers between devices, pieces(): far = lax.ppermute(crossing, 'fsdp', CHIP)  55.1 us
    pallas_call x1, Pallas kernels, ffn_call(): pl.pallas_call(ffn_kernel, out_shape=[jax.ShapeDtypeStruct((rows, model),...  44.2 us
    pallas_call x6, Pallas kernels, call(): pl.pallas_call(kernel, out_shape=[jax.ShapeDtypeStruct(forms[name][2], dt...  29.1 us
    all_gather x2, waiting for transfers between devices, layer(): gather = lambda a: lax.all_gather(a, 'fsdp', axis=0, tiled=True)  25.3 us
  transfers between devices with their start and end apart: 69, of which 32 were waited for; matrix products, arithmetic and copies ran while one was open for 8% of the time, Pallas kernels for 5%

profile of v1, /device:TPU:0, one launch (start us, length us, event | category | flops | bytes accessed | tf_op | source)
XLA Modules:
  0.0 593.2 jit_solution(12360619309595152314)
XLA Ops:
  9.5 6.0 %all_gather.10 = bf16[1024,2]{0,1:T(2,128)(2,1)S(1)} all-gather(bf16[256,2]{0,1:T(2,128)(2,1)S(1)} %pad_maximum_fusion.7), channel_id=1, replica_groups=mesh['ctx'=8,'fsdp'=4] {'fsdp'}, dimensions={0}, use_global_device_ids=true | all-gather | bytes 5120 | tf_op jit(solution)/shard_map/all_gather | solution.py:474
  16.1 25.3 %all-gather.3.cloned.1.call-done = bf16[1024,1536]{1,0:T(8,128)(2,1)} async-done(((bf16[256,1536]{1,0:T(8,128)(2,1)}), bf16[1024,1536]{1,0:T(8,128)(2,1)}) %all-gather.3.cloned.1.call-update) | async-done | bytes 3145744 | tf_op jit(solution)/shard_map/all_gather | solution.py:474
  41.4 3.7 convolution_convert_fusion
  51.0 15.6 %collective-permute-done = bf16[2,2,656,128]{3,2,1,0:T(8,128)(2,1)S(1)} collective-permute-done((bf16[2,2,656,128]{3,2,1,0:T(8,128)(2,1)S(1)}, bf16[2,2,656,128]{3,2,1,0:T(8,128)(2,1)S(1)}, u32[]{:S(2)}, u32[]{:S(2)}) %collective-permute-start) | collective-permute-done | bytes 671776 | tf_op jit(solution)/shard_map/ppermute | solution.py:462
  67.7 17.2 %collective-permute-done.1 = bf16[2,2,656,128]{3,2,1,0:T(8,128)(2,1)} collective-permute-done((bf16[2,2,656,128]{3,2,1,0:T(8,128)(2,1)S(1)}, bf16[2,2,656,128]{3,2,1,0:T(8,128)(2,1)}, u32[]{:S(2)}, u32[]{:S(2)}) %collective-permute-start.1) | collective-permute-done | bytes 671776 | tf_op jit(solution)/shard_map/ppermute | solution.py:462
  86.1 8.2 %collective-permute-done.5.refs_2_ = bf16[2752,256]{1,0:T(8,128)(2,1)} collective-permute-done((bf16[2752,256]{1,0:T(8,128)(2,1)}, bf16[2752,256]{1,0:T(8,128)(2,1)}, u32[]{:S(2)}, u32[]{:S(2)}) %collective-permute-start.5) | collective-permute-done | bytes 1409056 | tf_op jit(solution)/shard_map/ppermute | solution.py:400
  96.1 6.3 %collective-permute-done.2 = bf16[2,2,656,128]{3,2,1,0:T(8,128)(2,1)S(1)} collective-permute-done((bf16[2,2,656,128]{3,2,1,0:T(8,128)(2,1)}, bf16[2,2,656,128]{3,2,1,0:T(8,128)(2,1)S(1)}, u32[]{:S(2)}, u32[]{:S(2)}) %collective-permute-start.2) | collective-permute-done | bytes 671776 | tf_op jit(solution)/shard_map/ppermute | solution.py:462
  106.3 18.2 %collective-permute-done.8.refs_6_ = bf16[2752,256]{1,0:T(8,128)(2,1)} collective-permute-done((bf16[2752,256]{1,0:T(8,128)(2,1)}, bf16[2752,256]{1,0:T(8,128)(2,1)}, u32[]{:S(2)}, u32[]{:S(2)}) %collective-permute-start.8) | collective-permute-done | bytes 1409056 | tf_op jit(solution)/shard_map/ppermute | solution.py:400
  125.1 28.7 %collective-permute-done.11.refs_10_ = bf16[688,1024]{1,0:T(8,128)(2,1)} collective-permute-done((bf16[688,1024]{1,0:T(8,128)(2,1)}, bf16[688,1024]{1,0:T(8,128)(2,1)}, u32[]{:S(2)}, u32[]{:S(2)}) %collective-permute-start.11) | collective-permute-done | bytes 1409056 | tf_op jit(solution)/shard_map/ppermute | solution.py:400
  154.4 7.4 %shard_map.204 = (f32[1024,512]{1,0:T(8,128)S(1)}, f32[16,512]{1,0:T(8,128)S(1)}) custom-call(bf16[256,512]{1,0:T(8,128)(2,1)S(1)} %get-tuple-element.124.query_ref, bf16[256,512]{1,0:T(8,128)(2,1)S(1)} %get-tuple-element.123.key_ref, bf16[1024,512]{1,0:T(8,128)(2,1)S(1)} %slice.338.value_ref), custom_call_target="tpu_custom_call" | custom-call | flops 1073741824 | bytes 3145728 | tf_op jit(solution)/shard_map/pallas_call | solution.py:177
  164.2 2.6 shard_map.205
  166.8 4.4 convert_add_fusion.middle_ref
  171.3 44.2 %shard_map.206 = (bf16[512,1024]{1,0:T(8,128)(2,1)}, f32[512,1024]{1,0:T(8,128)}, bf16[512,1024]{1,0:T(8,128)(2,1)}, f32[8,1024]{1,0:T(8,128)}, bf16[2,2752,256]...) custom-call(s32[1]{0:T(128)} %bitcast.me_ref, ...), custom_call_target="tpu_custom_call" | custom-call | flops 25971130368 | bytes 39452672 | tf_op jit(solution)/shard_map/pallas_call | solution.py:288
  220.5 3.6 shard_map.207
  228.5 10.0 %shard_map.208 = (bf16[256,512]{1,0:T(8,128)(2,1)S(1)}, f32[256,512]{1,0:T(8,128)S(1)}, f32[1024,512]{1,0:T(8,128)S(1)}) custom-call(bf16[256,512]{1,0:T(8,128)(2,1)S(1)} %get-tuple-element.124.query_ref, bf16[256,512]{1,0:T(8,128)(2,1)S(1)} %get-tuple-element.123.key_ref, bf16[1024,512]{1,0:T(8,128)(2,1)S(1)} %slice.338.value_ref, ...), custom_call_target="tpu_custom_call" | custom-call | flops 2147483648 | bytes 6651904 | tf_op jit(solution)/shard_map/pallas_call | solution.py:177
  239.4 3.8 collective-permute-done.13
  246.2 15.0 %collective-permute-done.14 = bf16[2,2,656,128]{3,2,1,0:T(8,128)(2,1)S(1)} collective-permute-done((bf16[2,2,656,128]{3,2,1,0:T(8,128)(2,1)S(1)}, bf16[2,2,656,128]{3,2,1,0:T(8,128)(2,1)S(1)}, u32[]{:S(2)}, u32[]{:S(2)}) %collective-permute-start.14) | collective-permute-done | bytes 671776 | tf_op jit(solution)/shard_map/ppermute | solution.py:462
  261.4 4.4 collective-permute-start.31
  265.8 12.6 %collective-permute-done.30 = bf16[32,1024]{1,0:T(8,128)(2,1)S(1)} collective-permute-done((bf16[32,1024]{1,0:T(8,128)(2,1)S(1)}, bf16[32,1024]{1,0:T(8,128)(2,1)S(1)}, u32[]{:S(2)}, u32[]{:S(2)}) %collective-permute-start.30) | collective-permute-done | bytes 65568 | tf_op jit(solution)/shard_map/ppermute | solution.py:426
  278.4 2.8 collective-permute-done.31
  284.7 2.5 collective-permute-start.35
  294.9 6.2 %collective-permute-done.36 = bf16[128,1024]{1,0:T(8,128)(2,1)S(1)} collective-permute-done((bf16[128,1024]{1,0:T(8,128)(2,1)S(1)}, bf16[128,1024]{1,0:T(8,128)(2,1)S(1)}, u32[]{:S(2)}, u32[]{:S(2)}) %collective-permute-start.36) | collective-permute-done | bytes 262176 | tf_op jit(solution)/shard_map/ppermute | solution.py:426
  302.7 11.6 %collective-permute-done.16 = bf16[2,2,656,128]{3,2,1,0:T(8,128)(2,1)S(1)} collective-permute-done((bf16[2,2,656,128]{3,2,1,0:T(8,128)(2,1)S(1)}, bf16[2,2,656,128]{3,2,1,0:T(8,128)(2,1)S(1)}, u32[]{:S(2)}, u32[]{:S(2)}) %collective-permute-start.16) | collective-permute-done | bytes 671776 | tf_op jit(solution)/shard_map/ppermute | solution.py:466
  315.1 3.4 shard_map.209
  318.5 3.4 fusion.8
  323.2 3.2 shard_map.210
  337.4 25.0 %collective-permute-done.58 = bf16[688,1024]{1,0:T(8,128)(2,1)S(1)} collective-permute-done((bf16[688,1024]{1,0:T(8,128)(2,1)S(1)}, bf16[688,1024]{1,0:T(8,128)(2,1)S(1)}, u32[]{:S(2)}, u32[]{:S(2)}) %collective-permute-start.58) | collective-permute-done | bytes 1409056 | tf_op jit(solution)/shard_map/ppermute | solution.py:414
  366.3 26.3 %collective-permute-done.38 = bf16[2752,256]{1,0:T(8,128)(2,1)S(1)} collective-permute-done((bf16[2752,256]{1,0:T(8,128)(2,1)S(1)}, bf16[2752,256]{1,0:T(8,128)(2,1)S(1)}, u32[]{:S(2)}, u32[]{:S(2)}) %collective-permute-start.38) | collective-permute-done | bytes 1409056 | tf_op jit(solution)/shard_map/ppermute | solution.py:414
  396.0 26.3 %collective-permute-done.48 = bf16[2752,256]{1,0:T(8,128)(2,1)S(1)} collective-permute-done((bf16[2752,256]{1,0:T(8,128)(2,1)S(1)}, bf16[2752,256]{1,0:T(8,128)(2,1)S(1)}, u32[]{:S(2)}, u32[]{:S(2)}) %collective-permute-start.48) | collective-permute-done | bytes 1409056 | tf_op jit(solution)/shard_map/ppermute | solution.py:414
  429.5 12.2 %collective-permute-done.49 = bf16[1376,256]{1,0:T(8,128)(2,1)S(1)} collective-permute-done((bf16[1376,256]{1,0:T(8,128)(2,1)S(1)}, bf16[1376,256]{1,0:T(8,128)(2,1)S(1)}, u32[]{:S(2)}, u32[]{:S(2)}) %collective-permute-start.49) | collective-permute-done | bytes 704544 | tf_op jit(solution)/shard_map/ppermute | solution.py:426
  442.9 3.0 collective-permute-start.62
  446.0 5.0 collective-permute-done.42
  451.0 8.6 %collective-permute-start.50 = (bf16[344,256]{1,0:T(8,128)(2,1)S(1)}, bf16[344,256]{1,0:T(8,128)(2,1)S(1)}, u32[]{:S(2)}, u32[]{:S(2)}) collective-permute-start(bf16[344,256]{1,0:T(8,128)(2,1)S(1)} %get-tuple-element.128), channel_id=1, source_target_pairs={{0,8},{4,12},{8,0},{12,4},{16,24},{20,28},{24,16},{28,20},{1,9},{5... | collective-permute-start | bytes 528392 | tf_op jit(solution)/shard_map/ppermute | solution.py:426
  459.8 5.6 collective-permute-done.61
  466.2 3.1 collective-permute-start.43
  469.4 9.9 %collective-permute-start.44 = (bf16[344,256]{1,0:T(8,128)(2,1)S(1)}, bf16[344,256]{1,0:T(8,128)(2,1)S(1)}, u32[]{:S(2)}, u32[]{:S(2)}) collective-permute-start(bf16[344,256]{1,0:T(8,128)(2,1)S(1)} %add_convert_fusion.11), channel_id=1, source_target_pairs={{0,8},{4,12},{8,0},{12,4},{16,24},{20,28},{24,16},{28,20},{1,9},{5... | collective-permute-start | bytes 528392 | tf_op jit(solution)/shard_map/ppermute | solution.py:426
  480.7 4.0 collective-permute-done.51
  486.5 10.8 %collective-permute-start.64 = (bf16[688,128]{1,0:T(8,128)(2,1)S(1)}, bf16[688,128]{1,0:T(8,128)(2,1)S(1)}, u32[]{:S(2)}, u32[]{:S(2)}) collective-permute-start(bf16[688,128]{1,0:T(8,128)(2,1)S(1)} %add_convert_fusion.9), channel_id=1, source_target_pairs={{0,8},{4,12},{8,0},{12,4},{16,24},{20,28},{24,16},{28,20},{1,9},{5... | collective-permute-start | bytes 528392 | tf_op jit(solution)/shard_map/ppermute | solution.py:426
  497.4 5.8 collective-permute-done.45
  504.3 8.1 %collective-permute-start.20 = (bf16[32,1664]{1,0:T(8,128)(2,1)S(1)}, bf16[32,1664]{1,0:T(8,128)(2,1)S(1)}, u32[]{:S(2)}, u32[]{:S(2)}) collective-permute-start(bf16[32,1664]{1,0:T(8,128)(2,1)S(1)} %get-tuple-element.136), channel_id=1, source_target_pairs={{0,8},{4,12},{8,0},{12,4},{16,24},{20,28},{24,16},{28,20},{1,9},{5... | collective-permute-start | bytes 319496 | tf_op jit(solution)/shard_map/ppermute | solution.py:426
  512.6 8.4 %collective-permute-done.65 = bf16[688,128]{1,0:T(8,128)(2,1)S(1)} collective-permute-done((bf16[688,128]{1,0:T(8,128)(2,1)S(1)}, bf16[688,128]{1,0:T(8,128)(2,1)S(1)}, u32[]{:S(2)}, u32[]{:S(2)}) %collective-permute-start.65) | collective-permute-done | bytes 176160 | tf_op jit(solution)/shard_map/ppermute | solution.py:426
  521.2 10.0 %collective-permute-done.21 = bf16[32,1664]{1,0:T(8,128)(2,1)S(1)} collective-permute-done((bf16[32,1664]{1,0:T(8,128)(2,1)S(1)}, bf16[32,1664]{1,0:T(8,128)(2,1)S(1)}, u32[]{:S(2)}, u32[]{:S(2)}) %collective-permute-start.21) | collective-permute-done | bytes 106528 | tf_op jit(solution)/shard_map/ppermute | solution.py:426
  533.8 2.5 collective-permute-start.24
  541.4 3.0 collective-permute-done.25
  545.9 4.1 collective-permute-done.66
  550.6 14.5 %collective-permute-done.46 = bf16[1376,256]{1,0:T(8,128)(2,1)S(1)} collective-permute-done((bf16[1376,256]{1,0:T(8,128)(2,1)S(1)}, bf16[1376,256]{1,0:T(8,128)(2,1)S(1)}, u32[]{:S(2)}, u32[]{:S(2)}) %collective-permute-start.46) | collective-permute-done | bytes 704544 | tf_op jit(solution)/shard_map/ppermute | solution.py:426
  566.1 9.8 %collective-permute-done.56 = bf16[1376,256]{1,0:T(8,128)(2,1)S(1)} collective-permute-done((bf16[1376,256]{1,0:T(8,128)(2,1)S(1)}, bf16[1376,256]{1,0:T(8,128)(2,1)S(1)}, u32[]{:S(2)}, u32[]{:S(2)}) %collective-permute-start.56) | collective-permute-done | bytes 704544 | tf_op jit(solution)/shard_map/ppermute | solution.py:426
  577.0 2.9 convert_bitcast_fusion
  (310 shorter events, 98.3 us)
Async XLA Ops:
  7.2 34.2 %all-gather.3.cloned.1.call-start = ((), (), s32[]{:S(2)}) async-start(), calls=%async_computation | async-start | bytes 3932160 | tf_op jit(solution)/shard_map/all_gather | solution.py:474
  9.4 157.4 %all-gather.5.cloned.1.call-start = ((), (), s32[]{:S(2)}) async-start(), calls=%async_computation.1 | async-start | bytes 2621440 | tf_op jit(solution)/shard_map/all_gather | solution.py:474
  47.5 19.1 %collective-permute-start = (bf16[2,2,656,128]{3,2,1,0:T(8,128)(2,1)S(1)}, bf16[2,2,656,128]{3,2,1,0:T(8,128)(2,1)S(1)}, u32[]{:S(2)}, u32[]{:S(2)}) collective-permute-start(bf16[2,2,656,128]{3,2,1,0:T(8,128)(2,1)S(1)} %shard_map.203), channel_id=1, source_target_pairs={{0,8},{4,12},{8,16},{12,20},{16,24},{20,28},{24,0},{28,4},{1,9},{5... | collective-permute-start | bytes 2015240 | tf_op jit(solution)/shard_map/ppermute | solution.py:462
  49.1 45.3 %collective-permute-start.5 = (bf16[2752,256]{1,0:T(8,128)(2,1)}, bf16[2752,256]{1,0:T(8,128)(2,1)}, u32[]{:S(2)}, u32[]{:S(2)}) collective-permute-start(bf16[2752,256]{1,0:T(8,128)(2,1)} %bitcast.37.refs_0_), channel_id=1, source_target_pairs={{0,2},{2,0},{1,3},{3,1},{4,6},{6,4},{5,7},{7,5},{8,10},{10,8},{9,1... | collective-permute-start | bytes 4227080 | tf_op jit(solution)/shard_map/ppermute | solution.py:400
  49.6 56.1 %collective-permute-start.4 = (bf16[2752,256]{1,0:T(8,128)(2,1)}, bf16[2752,256]{1,0:T(8,128)(2,1)}, u32[]{:S(2)}, u32[]{:S(2)}) collective-permute-start(bf16[2752,256]{1,0:T(8,128)(2,1)} %bitcast.37.refs_0_), channel_id=1, source_target_pairs={{0,1},{1,0},{2,3},{3,2},{4,5},{5,4},{6,7},{7,6},{8,9},{9,8},{10,11... | collective-permute-start | bytes 4227080 | tf_op jit(solution)/shard_map/ppermute | solution.py:401
  66.6 18.3 %collective-permute-start.1 = (bf16[2,2,656,128]{3,2,1,0:T(8,128)(2,1)S(1)}, bf16[2,2,656,128]{3,2,1,0:T(8,128)(2,1)}, u32[]{:S(2)}, u32[]{:S(2)}) collective-permute-start(bf16[2,2,656,128]{3,2,1,0:T(8,128)(2,1)S(1)} %collective-permute-done), channel_id=1, source_target_pairs={{0,8},{4,12},{8,16},{12,20},{16,24},{20,28},{24,0},{28,4},{1,9},{5... | collective-permute-start | bytes 2015240 | tf_op jit(solution)/shard_map/ppermute | solution.py:462
  67.3 57.3 %collective-permute-start.8 = (bf16[2752,256]{1,0:T(8,128)(2,1)}, bf16[2752,256]{1,0:T(8,128)(2,1)}, u32[]{:S(2)}, u32[]{:S(2)}) collective-permute-start(bf16[2752,256]{1,0:T(8,128)(2,1)} %bitcast.38.refs_4_), channel_id=1, source_target_pairs={{0,2},{2,0},{1,3},{3,1},{4,6},{6,4},{5,7},{7,5},{8,10},{10,8},{9,1... | collective-permute-start | bytes 4227080 | tf_op jit(solution)/shard_map/ppermute | solution.py:400
  94.4 59.4 %collective-permute-start.11 = (bf16[688,1024]{1,0:T(8,128)(2,1)}, bf16[688,1024]{1,0:T(8,128)(2,1)}, u32[]{:S(2)}, u32[]{:S(2)}) collective-permute-start(bf16[688,1024]{1,0:T(8,128)(2,1)} %refs_8_.1), channel_id=1, source_target_pairs={{0,2},{2,0},{1,3},{3,1},{4,6},{6,4},{5,7},{7,5},{8,10},{10,8},{9,1... | collective-permute-start | bytes 4227080 | tf_op jit(solution)/shard_map/ppermute | solution.py:400
  104.2 20.4 %collective-permute-start.3 = (bf16[2,2,656,128]{3,2,1,0:T(8,128)(2,1)}, bf16[2,2,656,128]{3,2,1,0:T(8,128)(2,1)S(1)}, u32[]{:S(2)}, u32[]{:S(2)}) collective-permute-start(bf16[2,2,656,128]{3,2,1,0:T(8,128)(2,1)} %add_convert_fusion.7), channel_id=1, source_target_pairs={{0,4},{4,0},{8,12},{12,8},{16,20},{20,16},{24,28},{28,24},{1,5},{5... | collective-permute-start | bytes 2015240 | tf_op jit(solution)/shard_map/ppermute | solution.py:466
  105.7 65.5 %collective-permute-start.7 = (bf16[2752,256]{1,0:T(8,128)(2,1)}, bf16[2752,256]{1,0:T(8,128)(2,1)}, u32[]{:S(2)}, u32[]{:S(2)}) collective-permute-start(bf16[2752,256]{1,0:T(8,128)(2,1)} %bitcast.38.refs_4_), channel_id=1, source_target_pairs={{0,1},{1,0},{2,3},{3,2},{4,5},{5,4},{6,7},{7,6},{8,9},{9,8},{10,11... | collective-permute-start | bytes 4227080 | tf_op jit(solution)/shard_map/ppermute | solution.py:401
  105.7 65.5 %collective-permute-start.10 = (bf16[688,1024]{1,0:T(8,128)(2,1)}, bf16[688,1024]{1,0:T(8,128)(2,1)}, u32[]{:S(2)}, u32[]{:S(2)}) collective-permute-start(bf16[688,1024]{1,0:T(8,128)(2,1)} %refs_8_.1), channel_id=1, source_target_pairs={{0,1},{1,0},{2,3},{3,2},{4,5},{5,4},{6,7},{7,6},{8,9},{9,8},{10,11... | collective-permute-start | bytes 4227080 | tf_op jit(solution)/shard_map/ppermute | solution.py:401
  124.6 46.7 %collective-permute-start.6 = (bf16[2752,256]{1,0:T(8,128)(2,1)}, bf16[2752,256]{1,0:T(8,128)(2,1)}, u32[]{:S(2)}, u32[]{:S(2)}) collective-permute-start(bf16[2752,256]{1,0:T(8,128)(2,1)} %collective-permute-done.5.refs_2_), channel_id=1, source_target_pairs={{0,1},{1,0},{2,3},{3,2},{4,5},{5,4},{6,7},{7,6},{8,9},{9,8},{10,11... | collective-permute-start | bytes 4227080 | tf_op jit(solution)/shard_map/ppermute | solution.py:401
  124.6 46.7 %collective-permute-start.9 = (bf16[2752,256]{1,0:T(8,128)(2,1)}, bf16[2752,256]{1,0:T(8,128)(2,1)}, u32[]{:S(2)}, u32[]{:S(2)}) collective-permute-start(bf16[2752,256]{1,0:T(8,128)(2,1)} %collective-permute-done.8.refs_6_), channel_id=1, source_target_pairs={{0,1},{1,0},{2,3},{3,2},{4,5},{5,4},{6,7},{7,6},{8,9},{9,8},{10,11... | collective-permute-start | bytes 4227080 | tf_op jit(solution)/shard_map/ppermute | solution.py:401
  224.1 19.1 %collective-permute-start.13 = (bf16[2,2,656,128]{3,2,1,0:T(8,128)(2,1)}, bf16[2,2,656,128]{3,2,1,0:T(8,128)(2,1)S(1)}, u32[]{:S(2)}, u32[]{:S(2)}) collective-permute-start(bf16[2,2,656,128]{3,2,1,0:T(8,128)(2,1)} %get-tuple-element.53), channel_id=1, source_target_pairs={{0,8},{4,12},{8,16},{12,20},{16,24},{20,28},{24,0},{28,4},{1,9},{5... | collective-permute-start | bytes 2015240 | tf_op jit(solution)/shard_map/ppermute | solution.py:462
  227.3 99.3 %collective-permute-start.57 = (bf16[2,688,1024]{2,1,0:T(8,128)(2,1)}, bf16[2,688,1024]{2,1,0:T(8,128)(2,1)}, u32[]{:S(2)}, u32[]{:S(2)}) collective-permute-start(bf16[2,688,1024]{2,1,0:T(8,128)(2,1)} %get-tuple-element.68), channel_id=1, source_target_pairs={{0,1},{1,0},{2,3},{3,2},{4,5},{5,4},{6,7},{7,6},{8,9},{9,8},{10,11... | collective-permute-start | bytes 8454152 | tf_op jit(solution)/shard_map/ppermute | solution.py:412
  243.2 18.0 %collective-permute-start.14 = (bf16[2,2,656,128]{3,2,1,0:T(8,128)(2,1)S(1)}, bf16[2,2,656,128]{3,2,1,0:T(8,128)(2,1)S(1)}, u32[]{:S(2)}, u32[]{:S(2)}) collective-permute-start(bf16[2,2,656,128]{3,2,1,0:T(8,128)(2,1)S(1)} %collective-permute-done.13), channel_id=1, source_target_pairs={{0,8},{4,12},{8,16},{12,20},{16,24},{20,28},{24,0},{28,4},{1,9},{5... | collective-permute-start | bytes 2015240 | tf_op jit(solution)/shard_map/ppermute | solution.py:462
  261.2 32.2 %collective-permute-start.15 = (bf16[2,2,656,128]{3,2,1,0:T(8,128)(2,1)S(1)}, bf16[2,2,656,128]{3,2,1,0:T(8,128)(2,1)S(1)}, u32[]{:S(2)}, u32[]{:S(2)}) collective-permute-start(bf16[2,2,656,128]{3,2,1,0:T(8,128)(2,1)S(1)} %collective-permute-done.14), channel_id=1, source_target_pairs={{0,8},{4,12},{8,16},{12,20},{16,24},{20,28},{24,0},{28,4},{1,9},{5... | collective-permute-start | bytes 2015240 | tf_op jit(solution)/shard_map/ppermute | solution.py:462
  261.4 19.9 %collective-permute-start.31 = (bf16[32,1024]{1,0:T(8,128)(2,1)S(1)}, bf16[32,1024]{1,0:T(8,128)(2,1)S(1)}, u32[]{:S(2)}, u32[]{:S(2)}) collective-permute-start(bf16[32,1024]{1,0:T(8,128)(2,1)S(1)} %get-tuple-element.157), channel_id=1, source_target_pairs={{0,16},{4,20},{8,24},{12,28},{16,0},{20,4},{24,8},{28,12},{1,17},{... | collective-permute-start | bytes 196616 | tf_op jit(solution)/shard_map/ppermute | solution.py:426
  289.7 39.5 %collective-permute-start.37 = (bf16[2,2752,256]{2,1,0:T(8,128)(2,1)}, bf16[2,2752,256]{2,1,0:T(8,128)(2,1)}, u32[]{:S(2)}, u32[]{:S(2)}) collective-permute-start(bf16[2,2752,256]{2,1,0:T(8,128)(2,1)} %get-tuple-element.64), channel_id=1, source_target_pairs={{0,1},{1,0},{2,3},{3,2},{4,5},{5,4},{6,7},{7,6},{8,9},{9,8},{10,11... | collective-permute-start | bytes 8454152 | tf_op jit(solution)/shard_map/ppermute | solution.py:412
  289.7 45.0 %collective-permute-start.47 = (bf16[2,2752,256]{2,1,0:T(8,128)(2,1)}, bf16[2,2752,256]{2,1,0:T(8,128)(2,1)}, u32[]{:S(2)}, u32[]{:S(2)}) collective-permute-start(bf16[2,2752,256]{2,1,0:T(8,128)(2,1)} %get-tuple-element.66), channel_id=1, source_target_pairs={{0,1},{1,0},{2,3},{3,2},{4,5},{5,4},{6,7},{7,6},{8,9},{9,8},{10,11... | collective-permute-start | bytes 8454152 | tf_op jit(solution)/shard_map/ppermute | solution.py:412
  294.3 20.0 %collective-permute-start.16 = (bf16[2,2,656,128]{3,2,1,0:T(8,128)(2,1)S(1)}, bf16[2,2,656,128]{3,2,1,0:T(8,128)(2,1)S(1)}, u32[]{:S(2)}, u32[]{:S(2)}) collective-permute-start(bf16[2,2,656,128]{3,2,1,0:T(8,128)(2,1)S(1)} %add_convert_fusion.5), channel_id=1, source_target_pairs={{0,4},{4,0},{8,12},{12,8},{16,20},{20,16},{24,28},{28,24},{1,5},{5... | collective-permute-start | bytes 2015240 | tf_op jit(solution)/shard_map/ppermute | solution.py:466
  326.4 99.4 %collective-permute-start.17 = (bf16[2,256,1664]{2,1,0:T(8,128)(2,1)S(1)}, bf16[2,256,1664]{2,1,0:T(8,128)(2,1)S(1)}, u32[]{:S(2)}, u32[]{:S(2)}) collective-permute-start(bf16[2,256,1664]{2,1,0:T(8,128)(2,1)S(1)} %get-tuple-element.60), channel_id=1, source_target_pairs={{0,1},{1,0},{2,3},{3,2},{4,5},{5,4},{6,7},{7,6},{8,9},{9,8},{10,11... | collective-permute-start | bytes 5111816 | tf_op jit(solution)/shard_map/ppermute | solution.py:412
  328.7 33.7 %collective-permute-start.58 = (bf16[688,1024]{1,0:T(8,128)(2,1)S(1)}, bf16[688,1024]{1,0:T(8,128)(2,1)S(1)}, u32[]{:S(2)}, u32[]{:S(2)}) collective-permute-start(bf16[688,1024]{1,0:T(8,128)(2,1)S(1)} %fusion.17), channel_id=1, source_target_pairs={{0,2},{2,0},{1,3},{3,1},{4,6},{6,4},{5,7},{7,5},{8,10},{10,8},{9,1... | collective-permute-start | bytes 4227080 | tf_op jit(solution)/shard_map/ppermute | solution.py:414
  331.1 61.5 %collective-permute-start.38 = (bf16[2752,256]{1,0:T(8,128)(2,1)S(1)}, bf16[2752,256]{1,0:T(8,128)(2,1)S(1)}, u32[]{:S(2)}, u32[]{:S(2)}) collective-permute-start(bf16[2752,256]{1,0:T(8,128)(2,1)S(1)} %fusion.15), channel_id=1, source_target_pairs={{0,2},{2,0},{1,3},{3,1},{4,6},{6,4},{5,7},{7,5},{8,10},{10,8},{9,1... | collective-permute-start | bytes 4227080 | tf_op jit(solution)/shard_map/ppermute | solution.py:414
  336.9 85.4 %collective-permute-start.48 = (bf16[2752,256]{1,0:T(8,128)(2,1)S(1)}, bf16[2752,256]{1,0:T(8,128)(2,1)S(1)}, u32[]{:S(2)}, u32[]{:S(2)}) collective-permute-start(bf16[2752,256]{1,0:T(8,128)(2,1)S(1)} %fusion.16), channel_id=1, source_target_pairs={{0,2},{2,0},{1,3},{3,1},{4,6},{6,4},{5,7},{7,5},{8,10},{10,8},{9,1... | collective-permute-start | bytes 4227080 | tf_op jit(solution)/shard_map/ppermute | solution.py:414
  364.7 61.8 %collective-permute-start.59 = (bf16[688,512]{1,0:T(8,128)(2,1)S(1)}, bf16[688,512]{1,0:T(8,128)(2,1)S(1)}, u32[]{:S(2)}, u32[]{:S(2)}) collective-permute-start(bf16[688,512]{1,0:T(8,128)(2,1)S(1)} %dynamic-slice_convert_fusion), channel_id=1, source_target_pairs={{0,4},{4,0},{8,12},{12,8},{16,20},{20,16},{24,28},{28,24},{1,5},{5... | collective-permute-start | bytes 2113544 | tf_op jit(solution)/shard_map/ppermute | solution.py:426
  394.5 32.5 %collective-permute-start.39 = (bf16[1376,256]{1,0:T(8,128)(2,1)S(1)}, bf16[1376,256]{1,0:T(8,128)(2,1)S(1)}, u32[]{:S(2)}, u32[]{:S(2)}) collective-permute-start(bf16[1376,256]{1,0:T(8,128)(2,1)S(1)} %dynamic-slice_convert_fusion.2), channel_id=1, source_target_pairs={{0,4},{4,0},{8,12},{12,8},{16,20},{20,16},{24,28},{28,24},{1,5},{5... | collective-permute-start | bytes 2113544 | tf_op jit(solution)/shard_map/ppermute | solution.py:426
  426.0 43.3 %collective-permute-start.18 = (bf16[256,1664]{1,0:T(8,128)(2,1)S(1)}, bf16[256,1664]{1,0:T(8,128)(2,1)S(1)}, u32[]{:S(2)}, u32[]{:S(2)}) collective-permute-start(bf16[256,1664]{1,0:T(8,128)(2,1)S(1)} %fusion.18), channel_id=1, source_target_pairs={{0,2},{2,0},{1,3},{3,1},{4,6},{6,4},{5,7},{7,5},{8,10},{10,8},{9,1... | collective-permute-start | bytes 2555912 | tf_op jit(solution)/shard_map/ppermute | solution.py:414
  427.0 32.8 %collective-permute-start.60 = (bf16[688,128]{1,0:T(8,128)(2,1)S(1)}, bf16[688,128]{1,0:T(8,128)(2,1)S(1)}, u32[]{:S(2)}, u32[]{:S(2)}) collective-permute-start(bf16[688,128]{1,0:T(8,128)(2,1)S(1)} %get-tuple-element.125), channel_id=1, source_target_pairs={{0,8},{4,12},{8,0},{12,4},{16,24},{20,28},{24,16},{28,20},{1,9},{5... | collective-permute-start | bytes 528392 | tf_op jit(solution)/shard_map/ppermute | solution.py:426
  442.2 23.2 %collective-permute-start.61 = (bf16[688,128]{1,0:T(8,128)(2,1)S(1)}, bf16[688,128]{1,0:T(8,128)(2,1)S(1)}, u32[]{:S(2)}, u32[]{:S(2)}) collective-permute-start(bf16[688,128]{1,0:T(8,128)(2,1)S(1)} %get-tuple-element.127), channel_id=1, source_target_pairs={{0,16},{4,20},{8,24},{12,28},{16,0},{20,4},{24,8},{28,12},{1,17},{... | collective-permute-start | bytes 528392 | tf_op jit(solution)/shard_map/ppermute | solution.py:426
  442.9 23.3 %collective-permute-start.62 = (bf16[688,128]{1,0:T(8,128)(2,1)S(1)}, bf16[688,128]{1,0:T(8,128)(2,1)S(1)}, u32[]{:S(2)}, u32[]{:S(2)}) collective-permute-start(bf16[688,128]{1,0:T(8,128)(2,1)S(1)} %get-tuple-element.126), channel_id=1, source_target_pairs={{0,24},{4,28},{8,16},{12,20},{16,8},{20,12},{24,0},{28,4},{1,25},{... | collective-permute-start | bytes 528392 | tf_op jit(solution)/shard_map/ppermute | solution.py:426
  451.0 28.7 %collective-permute-start.50 = (bf16[344,256]{1,0:T(8,128)(2,1)S(1)}, bf16[344,256]{1,0:T(8,128)(2,1)S(1)}, u32[]{:S(2)}, u32[]{:S(2)}) collective-permute-start(bf16[344,256]{1,0:T(8,128)(2,1)S(1)} %get-tuple-element.128), channel_id=1, source_target_pairs={{0,8},{4,12},{8,0},{12,4},{16,24},{20,28},{24,16},{28,20},{1,9},{5... | collective-permute-start | bytes 528392 | tf_op jit(solution)/shard_map/ppermute | solution.py:426
  459.7 25.0 %collective-permute-start.51 = (bf16[344,256]{1,0:T(8,128)(2,1)S(1)}, bf16[344,256]{1,0:T(8,128)(2,1)S(1)}, u32[]{:S(2)}, u32[]{:S(2)}) collective-permute-start(bf16[344,256]{1,0:T(8,128)(2,1)S(1)} %get-tuple-element.130), channel_id=1, source_target_pairs={{0,16},{4,20},{8,24},{12,28},{16,0},{20,4},{24,8},{28,12},{1,17},{... | collective-permute-start | bytes 528392 | tf_op jit(solution)/shard_map/ppermute | solution.py:426
  465.4 19.5 %collective-permute-start.52 = (bf16[344,256]{1,0:T(8,128)(2,1)S(1)}, bf16[344,256]{1,0:T(8,128)(2,1)S(1)}, u32[]{:S(2)}, u32[]{:S(2)}) collective-permute-start(bf16[344,256]{1,0:T(8,128)(2,1)S(1)} %get-tuple-element.129), channel_id=1, source_target_pairs={{0,24},{4,28},{8,16},{12,20},{16,8},{20,12},{24,0},{28,4},{1,25},{... | collective-permute-start | bytes 528392 | tf_op jit(solution)/shard_map/ppermute | solution.py:426
  466.2 20.3 %collective-permute-start.43 = (bf16[344,256]{1,0:T(8,128)(2,1)S(1)}, bf16[344,256]{1,0:T(8,128)(2,1)S(1)}, u32[]{:S(2)}, u32[]{:S(2)}) collective-permute-start(bf16[344,256]{1,0:T(8,128)(2,1)S(1)} %add_convert_fusion.11), channel_id=1, source_target_pairs={{0,24},{4,28},{8,16},{12,20},{16,8},{20,12},{24,0},{28,4},{1,25},{... | collective-permute-start | bytes 528392 | tf_op jit(solution)/shard_map/ppermute | solution.py:426
  469.4 28.0 %collective-permute-start.44 = (bf16[344,256]{1,0:T(8,128)(2,1)S(1)}, bf16[344,256]{1,0:T(8,128)(2,1)S(1)}, u32[]{:S(2)}, u32[]{:S(2)}) collective-permute-start(bf16[344,256]{1,0:T(8,128)(2,1)S(1)} %add_convert_fusion.11), channel_id=1, source_target_pairs={{0,8},{4,12},{8,0},{12,4},{16,24},{20,28},{24,16},{28,20},{1,9},{5... | collective-permute-start | bytes 528392 | tf_op jit(solution)/shard_map/ppermute | solution.py:426
  479.7 23.5 %collective-permute-start.45 = (bf16[344,256]{1,0:T(8,128)(2,1)S(1)}, bf16[344,256]{1,0:T(8,128)(2,1)S(1)}, u32[]{:S(2)}, u32[]{:S(2)}) collective-permute-start(bf16[344,256]{1,0:T(8,128)(2,1)S(1)} %add_convert_fusion.11), channel_id=1, source_target_pairs={{0,16},{4,20},{8,24},{12,28},{16,0},{20,4},{24,8},{28,12},{1,17},{... | collective-permute-start | bytes 528392 | tf_op jit(solution)/shard_map/ppermute | solution.py:426
  484.7 19.6 %collective-permute-start.63 = (bf16[688,128]{1,0:T(8,128)(2,1)S(1)}, bf16[688,128]{1,0:T(8,128)(2,1)S(1)}, u32[]{:S(2)}, u32[]{:S(2)}) collective-permute-start(bf16[688,128]{1,0:T(8,128)(2,1)S(1)} %add_convert_fusion.9), channel_id=1, source_target_pairs={{0,24},{4,28},{8,16},{12,20},{16,8},{20,12},{24,0},{28,4},{1,25},{... | collective-permute-start | bytes 528392 | tf_op jit(solution)/shard_map/ppermute | solution.py:426
  485.0 19.1 %collective-permute-start.19 = (bf16[128,1664]{1,0:T(8,128)(2,1)S(1)}, bf16[128,1664]{1,0:T(8,128)(2,1)S(1)}, u32[]{:S(2)}, u32[]{:S(2)}) collective-permute-start(bf16[128,1664]{1,0:T(8,128)(2,1)S(1)} %dynamic-slice_convert_fusion.3), channel_id=1, source_target_pairs={{0,4},{4,0},{8,12},{12,8},{16,20},{20,16},{24,28},{28,24},{1,5},{5... | collective-permute-start | bytes 1277960 | tf_op jit(solution)/shard_map/ppermute | solution.py:426
  486.5 25.9 %collective-permute-start.64 = (bf16[688,128]{1,0:T(8,128)(2,1)S(1)}, bf16[688,128]{1,0:T(8,128)(2,1)S(1)}, u32[]{:S(2)}, u32[]{:S(2)}) collective-permute-start(bf16[688,128]{1,0:T(8,128)(2,1)S(1)} %add_convert_fusion.9), channel_id=1, source_target_pairs={{0,8},{4,12},{8,0},{12,4},{16,24},{20,28},{24,16},{28,20},{1,9},{5... | collective-permute-start | bytes 528392 | tf_op jit(solution)/shard_map/ppermute | solution.py:426
  497.4 23.6 %collective-permute-start.65 = (bf16[688,128]{1,0:T(8,128)(2,1)S(1)}, bf16[688,128]{1,0:T(8,128)(2,1)S(1)}, u32[]{:S(2)}, u32[]{:S(2)}) collective-permute-start(bf16[688,128]{1,0:T(8,128)(2,1)S(1)} %add_convert_fusion.9), channel_id=1, source_target_pairs={{0,16},{4,20},{8,24},{12,28},{16,0},{20,4},{24,8},{28,12},{1,17},{... | collective-permute-start | bytes 528392 | tf_op jit(solution)/shard_map/ppermute | solution.py:426
  503.2 30.1 %collective-permute-start.53 = (bf16[344,256]{1,0:T(8,128)(2,1)S(1)}, bf16[344,256]{1,0:T(8,128)(2,1)S(1)}, u32[]{:S(2)}, u32[]{:S(2)}) collective-permute-start(bf16[344,256]{1,0:T(8,128)(2,1)S(1)} %add_convert_fusion.10), channel_id=1, source_target_pairs={{0,24},{4,28},{8,16},{12,20},{16,8},{20,12},{24,0},{28,4},{1,25},{... | collective-permute-start | bytes 528392 | tf_op jit(solution)/shard_map/ppermute | solution.py:426
  504.1 29.7 %collective-permute-start.54 = (bf16[344,256]{1,0:T(8,128)(2,1)S(1)}, bf16[344,256]{1,0:T(8,128)(2,1)S(1)}, u32[]{:S(2)}, u32[]{:S(2)}) collective-permute-start(bf16[344,256]{1,0:T(8,128)(2,1)S(1)} %add_convert_fusion.10), channel_id=1, source_target_pairs={{0,8},{4,12},{8,0},{12,4},{16,24},{20,28},{24,16},{28,20},{1,9},{5... | collective-permute-start | bytes 528392 | tf_op jit(solution)/shard_map/ppermute | solution.py:426
  512.5 18.7 %collective-permute-start.21 = (bf16[32,1664]{1,0:T(8,128)(2,1)S(1)}, bf16[32,1664]{1,0:T(8,128)(2,1)S(1)}, u32[]{:S(2)}, u32[]{:S(2)}) collective-permute-start(bf16[32,1664]{1,0:T(8,128)(2,1)S(1)} %get-tuple-element.138), channel_id=1, source_target_pairs={{0,16},{4,20},{8,24},{12,28},{16,0},{20,4},{24,8},{28,12},{1,17},{... | collective-permute-start | bytes 319496 | tf_op jit(solution)/shard_map/ppermute | solution.py:426
  531.2 18.7 %collective-permute-start.66 = (bf16[688,512]{1,0:T(8,128)(2,1)S(1)}, bf16[688,512]{1,0:T(8,128)(2,1)S(1)}, u32[]{:S(2)}, u32[]{:S(2)}) collective-permute-start(bf16[688,512]{1,0:T(8,128)(2,1)S(1)} %pad_maximum_fusion.3), channel_id=1, source_target_pairs={{0,4},{4,0},{8,12},{12,8},{16,20},{20,16},{24,28},{28,24},{1,5},{5... | collective-permute-start | bytes 2113544 | tf_op jit(solution)/shard_map/ppermute | solution.py:426
  532.7 32.4 %collective-permute-start.46 = (bf16[1376,256]{1,0:T(8,128)(2,1)S(1)}, bf16[1376,256]{1,0:T(8,128)(2,1)S(1)}, u32[]{:S(2)}, u32[]{:S(2)}) collective-permute-start(bf16[1376,256]{1,0:T(8,128)(2,1)S(1)} %pad_maximum_fusion.1), channel_id=1, source_target_pairs={{0,4},{4,0},{8,12},{12,8},{16,20},{20,16},{24,28},{28,24},{1,5},{5... | collective-permute-start | bytes 2113544 | tf_op jit(solution)/shard_map/ppermute | solution.py:426
  540.0 35.9 %collective-permute-start.56 = (bf16[1376,256]{1,0:T(8,128)(2,1)S(1)}, bf16[1376,256]{1,0:T(8,128)(2,1)S(1)}, u32[]{:S(2)}, u32[]{:S(2)}) collective-permute-start(bf16[1376,256]{1,0:T(8,128)(2,1)S(1)} %pad_maximum_fusion.2), channel_id=1, source_target_pairs={{0,4},{4,0},{8,12},{12,8},{16,20},{20,16},{24,28},{28,24},{1,5},{5... | collective-permute-start | bytes 2113544 | tf_op jit(solution)/shard_map/ppermute | solution.py:426
  544.4 38.2 %collective-permute-start.26 = (bf16[128,1664]{1,0:T(8,128)(2,1)S(1)}, bf16[128,1664]{1,0:T(8,128)(2,1)S(1)}, u32[]{:S(2)}, u32[]{:S(2)}) collective-permute-start(bf16[128,1664]{1,0:T(8,128)(2,1)S(1)} %pad_maximum_fusion.4), channel_id=1, source_target_pairs={{0,4},{4,0},{8,12},{12,8},{16,20},{20,16},{24,28},{28,24},{1,5},{5... | collective-permute-start | bytes 1277960 | tf_op jit(solution)/shard_map/ppermute | solution.py:426
  (61 other events, 630.2 us)
Sparse Core Ops, SparseCore 0:
  10.2 31.2 all-gather.2
  49.8 34.0 all-gather.4

commit v2 on v1

--- a/solution.py
+++ b/solution.py
@@ -194,17 +194,13 @@
     return (step % 2) * 2 + step // 2
 
 
-def ffn_kernel(me_ref, middle_ref, gain_ref, cot_ref, *refs):
-    gates, ups, downs = refs[:4], refs[4:8], refs[8:12]
-    output_ref, gmiddle_ref, branch_ref, ggain_ref = refs[12:16]
-    gate_keep, gate_send, up_keep, up_send, down_keep, down_send = refs[16:22]
-    normed, x_own, x_turned, cot_turned, down, total, gnormed = refs[22:]
+def ffn_kernel(me_ref, middle_ref, gain_ref, cot_ref, gates, ups, downs, *refs):
+    output_ref, gmiddle_ref, branch_ref, ggain_ref = refs[:4]
+    gate_keep, gate_send, up_keep, up_send, down_keep, down_send = refs[4:10]
+    normed, x_own, x_turned, cot_turned, total, gnormed = refs[10:]
     step = pl.program_id(0)
     me = me_ref[0]
-    width = gates[0].shape[1]
-
-    def columns(r):
-        return pl.ds(pl.multiple_of((me ^ r) * width, width), width)
+    width = gates.shape[2]
 
     def inverse():
         middle = middle_ref[...]
@@ -214,32 +210,27 @@
     def _():
         normed[...] = (middle_ref[...] * inverse() * gain_ref[...]).astype(bf16)
         for r in range(4):
-            part = normed[:, columns(r)]
-            x_own[:, r * width : (r + 1) * width] = part
-            x_turned[r * width : (r + 1) * width, :] = part.T
+            x_own[r] = normed[:, pl.ds(pl.multiple_of((me ^ r) * width, width), width)]
+        x_turned[...] = normed[...].T
         cot_turned[...] = cot_ref[...].T
         total[...] = jnp.zeros_like(total)
         gnormed[...] = jnp.zeros_like(gnormed)
 
-    for at in range(4):
-
-        @pl.when(step == at)
-        def _(at=at):
-            down[...] = downs[ORDER[at]][...]
-
-    gate = dot(gates[0][...], x_turned[:width, :], (1, 0))
-    up = dot(ups[0][...], x_turned[:width, :], (1, 0))
+    x_part = x_turned[:width, :]
+    gate = dot(gates[0], x_part, (1, 0))
+    up = dot(ups[0], x_part, (1, 0))
     for r in range(1, 4):
         x_part = x_turned[r * width : (r + 1) * width, :]
-        gate = gate + dot(gates[r][...], x_part, (1, 0))
-        up = up + dot(ups[r][...], x_part, (1, 0))
-    ghidden = dot(down[...], cot_turned[...], (1, 0))
+        gate = gate + dot(gates[r], x_part, (1, 0))
+        up = up + dot(ups[r], x_part, (1, 0))
+    down = downs[0]
+    ghidden = dot(down, cot_turned[...], (1, 0))
     sigmoid = jax.nn.sigmoid(gate)
     silu = gate * sigmoid
     hidden = (silu * up).astype(bf16)
     ggate = (ghidden * up * (sigmoid * (1.0 + gate * (1.0 - sigmoid)))).astype(bf16)
     gup = (ghidden * silu).astype(bf16)
-    total[...] += dot(hidden, down[...], (0, 0))
+    total[...] += dot(hidden, down, (0, 0))
     gdown = dot(hidden, cot_ref[...], (1, 0)).astype(bf16)
 
     @pl.when(step < 2)
@@ -252,17 +243,14 @@
 
     for r in range(4):
         part = slice(r * width, (r + 1) * width)
-        gnormed[:, part] += dot(ggate, gates[r][...], (0, 0)) + dot(gup, ups[r][...], (0, 0))
-        x_part = x_own[:, part]
-        (gate_send if r % 2 else gate_keep)[r // 2] = dot(ggate, x_part, (1, 0)).astype(bf16)
-        (up_send if r % 2 else up_keep)[r // 2] = dot(gup, x_part, (1, 0)).astype(bf16)
+        gnormed[:, part] += dot(ggate, gates[r], (0, 0)) + dot(gup, ups[r], (0, 0))
+        (gate_send if r % 2 else gate_keep)[r // 2] = dot(ggate, x_own[r], (1, 0)).astype(bf16)
+        (up_send if r % 2 else up_keep)[r // 2] = dot(gup, x_own[r], (1, 0)).astype(bf16)
 
     @pl.when(step == 3)
     def _():
-        for r in range(4):
-            gmiddle_ref[:, columns(r)] = gnormed[:, r * width : (r + 1) * width]
         middle, inv, cot = middle_ref[...], inverse(), cot_ref[...].astype(f32)
-        grad = gmiddle_ref[...]
+        grad = gnormed[...]
         output_ref[...] = (middle + total[...]).astype(bf16)
         ggain_ref[...] = jnp.broadcast_to(jnp.sum(grad * middle * inv, axis=0, keepdims=True), ggain_ref.shape)
         weighted = grad * gain_ref[...]
@@ -274,14 +262,14 @@
 
 def ffn_call(me, middle, gain, cot, gates, ups, downs):
     rows, model = middle.shape
-    hidden, width = gates[0].shape
-    tile = downs[0].shape[0]
+    _, hidden, width = gates.shape
+    tile = downs.shape[1]
     once = pl.Buffered(1)
 
     def whole(shape, **kw):
         return pl.BlockSpec(shape, lambda s, me: (0,) * len(shape), **kw)
 
-    piece = pl.BlockSpec((tile, width), lambda s, me: (me[0] ^ place(s), 0))
+    columns = pl.BlockSpec((4, tile, width), lambda s, me: (0, me[0] ^ place(s), 0))
     pair = pl.BlockSpec((2, tile, width), lambda s, me: (0, me[0] ^ place(s), 0))
     pair_shape = jax.ShapeDtypeStruct((2, hidden, width), bf16)
     down_shape = jax.ShapeDtypeStruct((2, tile, model), bf16)
@@ -302,9 +290,14 @@
         grid_spec=pltpu.PrefetchScalarGridSpec(
             num_scalar_prefetch=1,
             grid=(4,),
-            in_specs=[whole((rows, model), pipeline_mode=once), whole((1, model)), whole((rows, model), pipeline_mode=once)]
-            + [piece] * 8
-            + [whole((tile, model), pipeline_mode=once)] * 4,
+            in_specs=[
+                whole((rows, model), pipeline_mode=once),
+                whole((1, model)),
+                whole((rows, model), pipeline_mode=once),
+                columns,
+                columns,
+                pl.BlockSpec((1, tile, model), lambda s, me: (me[0] ^ place(s), 0, 0)),
+            ],
             out_specs=[
                 whole((rows, model), pipeline_mode=once),
                 whole((rows, model), pipeline_mode=once),
@@ -319,10 +312,9 @@
             ],
             scratch_shapes=[
                 pltpu.VMEM((rows, model), bf16),
-                pltpu.VMEM((rows, model), bf16),
+                pltpu.VMEM((4, rows, width), bf16),
                 pltpu.VMEM((model, rows), bf16),
                 pltpu.VMEM((model, rows), bf16),
-                pltpu.VMEM((tile, model), bf16),
                 pltpu.VMEM((rows, model), f32),
                 pltpu.VMEM((rows, model), f32),
             ],
@@ -331,7 +323,7 @@
         cost_estimate=pl.CostEstimate(
             flops=18 * rows * model * hidden, bytes_accessed=14 * hidden * model, transcendentals=0
         ),
-    )(me, middle, gain, cot, *gates, *ups, *downs)
+    )(me, middle, gain, cot, gates, ups, downs)
 
 
 def out_grad_kernel(me_ref, atten_ref, branch_ref, keep_ref, send_ref):
@@ -395,10 +387,21 @@
 CHIP = [(0, 2), (2, 0), (1, 3), (3, 1)]
 
 
-def pieces(shard, after=None):
-    crossing = shard if after is None else lax.optimization_barrier((shard, after))[0]
-    far = lax.ppermute(crossing, "fsdp", CHIP)
-    return shard, lax.ppermute(shard, "fsdp", CORE), far, lax.ppermute(far, "fsdp", CORE)
+class Links:
+    def __init__(self):
+        self.last = ()
+
+    def round(self, sends, beside=()):
+        arrays = [send[0] for send in sends]
+        if self.last:
+            arrays = lax.optimization_barrier((*arrays, *self.last))[: len(arrays)]
+        results = [lax.ppermute(a, axis, perm) for a, (_, axis, perm) in zip(arrays, sends)]
+        self.last = (*results, *beside)
+        return results
+
+
+def trade(array, bits, count):
+    return array, "ctx", [(i, i ^ bits) for i in range(count)]
 
 
 def ordered(parts, place_bits):
@@ -408,35 +411,261 @@
     return parts
 
 
-def summed(keep, send, own, count, axis):
-    got = lax.ppermute(send, "fsdp", CORE)
-    cross = (keep[1].astype(f32) + got[1].astype(f32)).astype(bf16)
-    got_cross = lax.ppermute(cross, "fsdp", CHIP)
-    total = keep[0].astype(f32) + got[0].astype(f32) + got_cross.astype(f32)
-    if count != 8:
-        return lax.psum(total.astype(bf16), "ctx").astype(f32)
-    size = total.shape[axis]
-    y, z = own % 2, own // 2
-
-    def cut(array, index, parts):
-        part = array.shape[axis] // parts
-        return lax.dynamic_slice_in_dim(array, index * part, part, axis)
-
-    def trade(array, bits):
-        return lax.ppermute(array, "ctx", [(i, i ^ bits) for i in range(count)])
-
-    got_half = trade(cut(total, 1 - y, 2).astype(bf16), 1)
-    half = cut(total, y, 2) + got_half.astype(f32)
-    mine = cut(half, z, 4)
-    for k in (1, 2, 3):
-        mine = mine + trade(cut(half, z ^ k, 4).astype(bf16), 2 * k).astype(f32)
-    mine = mine.astype(bf16)
-    near = [mine] + [trade(mine, 2 * k) for k in (1, 2, 3)]
-    far = trade(jnp.concatenate(near, axis=axis), 1)
-    far = [cut(far, k, 4) for k in range(4)]
-    low = [jnp.where(y == 0, a, b) for a, b in zip(near, far)]
-    high = [jnp.where(y == 0, b, a) for a, b in zip(near, far)]
-    return jnp.concatenate(ordered(low, z) + ordered(high, z), axis=axis).astype(f32)
+def cut(array, index, parts, axis):
+    part = array.shape[axis] // parts
+    return lax.dynamic_slice_in_dim(array, index * part, part, axis)
+
+
+MESH = pl.DeviceIdType.MESH
+
+
+class Spot:
+    def __init__(self):
+        self.me = lax.axis_index("fsdp")
+        self.own = lax.axis_index("ctx")
+        self.core = {"fsdp": self.me + 1 - 2 * (self.me % 2)}
+        self.across = (self.me + 2) % 4
+        self.chip = {"fsdp": self.across}
+        self.y = self.own % 2
+        self.z = self.own // 2
+        self.side = {"ctx": self.own + 1 - 2 * self.y}
+        self.ahead = [None] + [{"ctx": (self.own + 2 * k) % 8} for k in (1, 2, 3)]
+
+    def greet(self, neighbours):
+        barrier = pltpu.get_barrier_semaphore()
+        for neighbour in neighbours:
+            pl.semaphore_signal(barrier, inc=1, device_id=neighbour, device_id_type=MESH)
+        pl.semaphore_wait(barrier, len(neighbours))
+
+
+class Wire:
+    def __init__(self, send_sems, recv_sems, local_sems):
+        self.send_sems, self.recv_sems, self.local_sems = send_sems, recv_sems, local_sems
+        self.sent, self.local = [], []
+
+    def send(self, source, target, device):
+        k = len(self.sent)
+        copy = pltpu.make_async_remote_copy(
+            src_ref=source,
+            dst_ref=target,
+            send_sem=self.send_sems.at[k],
+            recv_sem=self.recv_sems.at[k],
+            device_id=device,
+            device_id_type=MESH,
+        )
+        copy.start()
+        self.sent.append(copy)
+        return copy
+
+    def keep(self, source, target):
+        copy = pltpu.make_async_copy(source, target, self.local_sems.at[len(self.local)])
+        copy.start()
+        self.local.append(copy)
+        return copy
+
+    def end(self):
+        for copy in self.sent:
+            copy.wait_send()
+
+
+class Gather:
+    def __init__(self, wire, spot, shard, full, axis):
+        self.wire, self.spot, self.full, self.axis = wire, spot, full, axis
+        me = spot.me
+        self.own = wire.keep(shard, full.at[me])
+        self.cross = wire.send(self.half(shard, spot.y), self.half(full.at[me], spot.y), spot.chip)
+        self.near = wire.send(shard, full.at[me], spot.core)
+
+    def half(self, ref, y):
+        size = ref.shape[self.axis] // 2
+        index = [slice(None)] * 2
+        index[self.axis] = pl.ds(pl.multiple_of(y * size, size), size)
+        return ref.at[tuple(index)]
+
+    def relay(self):
+        self.cross.wait_recv()
+        part = self.half(self.full.at[self.spot.across], self.spot.y)
+        self.side = self.wire.send(part, part, self.spot.side)
+        self.far = [self.wire.send(part, part, self.spot.core)]
+
+    def relay_other(self):
+        self.side.wait_recv()
+        part = self.half(self.full.at[self.spot.across], 1 - self.spot.y)
+        self.far.append(self.wire.send(part, part, self.spot.core))
+
+    def end(self):
+        self.own.wait()
+        self.near.wait_recv()
+        for copy in self.far:
+            copy.wait_recv()
+
+
+def gather_kernel(gain_ref, in_ref, gain_full, in_full, send_sems, recv_sems, local_sems):
+    spot = Spot()
+    wire = Wire(send_sems, recv_sems, local_sems)
+    spot.greet([spot.core, spot.chip, spot.side])
+    own = wire.keep(gain_ref, gain_full.at[spot.me])
+    near = wire.send(gain_ref, gain_full.at[spot.me], spot.core)
+    cross = wire.send(gain_ref, gain_full.at[spot.me], spot.chip)
+    weight = Gather(wire, spot, in_ref, in_full, 0)
+    cross.wait_recv()
+    far = wire.send(gain_full.at[spot.across], gain_full.at[spot.across], spot.core)
+    weight.relay()
+    weight.relay_other()
+    own.wait()
+    near.wait_recv()
+    far.wait_recv()
+    weight.end()
+    wire.end()
+
+
+def add_masked(total, piece, mask_ref, source, block, first):
+    for group in range(piece.shape[0]):
+        states = piece[group].astype(f32)
+        for target in range(4):
+            term = states * mask_ref[target, 2 * source + block]
+            if first:
+                total[target, group] = term
+            else:
+                total[target, group] += term
+
+
+def forward_kernel(
+    mask_ref, states_ref, query_ref, key_ref, value_ref, *refs
+):
+    weights, (prefix_ref, numer_ref, denom_ref), fulls = refs[:4], refs[4:7], refs[7:11]
+    ring, total, outgoing, incoming, send_sems, recv_sems, local_sems = refs[11:]
+    spot = Spot()
+    wire = Wire(send_sems, recv_sems, local_sems)
+    spot.greet([spot.core, spot.chip, spot.side, spot.ahead[1], spot.ahead[3]])
+    hops = [[wire.send(states_ref.at[b], ring.at[0, b], spot.ahead[1]) for b in range(2)]]
+    gathers = [Gather(wire, spot, w, full, axis) for w, full, axis in zip(weights, fulls, (0, 0, 0, 1))]
+    for block in range(2):
+        for group in range(HEADS // GROUP):
+            narrow = (slice(group * GROUP * FDIM, (group + 1) * GROUP * FDIM), slice(block * BLOCK, (block + 1) * BLOCK))
+            wide = (slice(group * GROUP * VDIM, (group + 1) * GROUP * VDIM), narrow[1])
+            heads = (slice(group * GROUP, (group + 1) * GROUP), narrow[1])
+            intra_kernel(
+                query_ref.at[narrow], key_ref.at[narrow], value_ref.at[wide], numer_ref.at[wide], denom_ref.at[heads]
+            )
+            if group == 1:
+                hops[0][block].wait_recv()
+                hops.append([]) if block == 0 else None
+                hops[1].append(wire.send(ring.at[0, block], ring.at[1, block], spot.ahead[1]))
+            if (block, group) == (1, 0):
+                gathers[0].relay()
+    for block in range(2):
+        add_masked(total, states_ref.at[block], mask_ref, 0, block, block == 0)
+        add_masked(total, ring.at[0, block], mask_ref, 1, block, False)
+    gathers[1].relay()
+    gathers[0].relay_other()
+    hops.append([])
+    for block in range(2):
+        hops[1][block].wait_recv()
+        hops[2].append(wire.send(ring.at[1, block], ring.at[2, block], spot.ahead[1]))
+        add_masked(total, ring.at[1, block], mask_ref, 2, block, False)
+    gathers[2].relay()
+    gathers[1].relay_other()
+    for block in range(2):
+        hops[2][block].wait_recv()
+        add_masked(total, ring.at[2, block], mask_ref, 3, block, False)
+    outgoing[...] = total[2:].astype(bf16)
+    partner = wire.send(outgoing, incoming, spot.side)
+    gathers[3].relay()
+    gathers[2].relay_other()
+    partner.wait_recv()
+    prefix_ref[...] = (total[:2] + incoming[...].astype(f32)).astype(bf16)
+    gathers[3].relay_other()
+    for one in gathers:
+        one.end()
+    wire.end()
+
+
+HBM = pl.BlockSpec(memory_space=pltpu.HBM)
+VMEM = pl.BlockSpec(memory_space=pltpu.VMEM)
+SMEM = pl.BlockSpec(memory_space=pltpu.SMEM)
+
+
+def sems(count):
+    return pltpu.SemaphoreType.DMA((count,))
+
+
+def gather_call(gains, in_shard):
+    return pl.pallas_call(
+        gather_kernel,
+        out_shape=[jax.ShapeDtypeStruct((4, *a.shape), a.dtype) for a in (gains, in_shard)],
+        in_specs=[HBM, HBM],
+        out_specs=[HBM, HBM],
+        scratch_shapes=[sems(8), sems(8), sems(2)],
+        compiler_params=pltpu.CompilerParams(collective_id=0, has_side_effects=True, vmem_limit_bytes=16 << 20),
+    )(gains, in_shard)
+
+
+def forward_call(masks, states, query, key, value, weights):
+    state = states.shape
+    rows = query.shape[1]
+    return pl.pallas_call(
+        forward_kernel,
+        out_shape=[
+            jax.ShapeDtypeStruct(state, bf16),
+            jax.ShapeDtypeStruct((HEADS * VDIM, rows), f32),
+            jax.ShapeDtypeStruct((HEADS, rows), f32),
+        ]
+        + [jax.ShapeDtypeStruct((4, *w.shape), bf16) for w in weights],
+        in_specs=[SMEM, VMEM, VMEM, VMEM, VMEM] + [HBM] * 4,
+        out_specs=[VMEM, VMEM, VMEM] + [HBM] * 4,
+        scratch_shapes=[
+            pltpu.VMEM((3, *state), bf16),
+            pltpu.VMEM((4, *state[1:]), f32),
+            pltpu.VMEM(state, bf16),
+            pltpu.VMEM(state, bf16),
+            sems(28),
+            sems(28),
+            sems(4),
+        ],
+        compiler_params=pltpu.CompilerParams(collective_id=1, has_side_effects=True, vmem_limit_bytes=40 << 20),
+    )(masks, states, query, key, value, *weights)
+
+
+class Shard:
+    def __init__(self, keep, send, own, rows, y_axis, z_axis):
+        self.keep, self.whole_send, self.rows = keep, send, rows
+        self.y, self.z, self.y_axis, self.z_axis = own % 2, own // 2, y_axis, z_axis
+
+    def cross(self, got):
+        start, stop = self.rows
+        self.got = got
+        return (self.keep[1, start:stop].astype(f32) + got[1, start:stop].astype(f32)).astype(bf16), "fsdp", CHIP
+
+    def chip_sum(self, got_cross):
+        start, stop = self.rows
+        return self.keep[0, start:stop].astype(f32) + self.got[0, start:stop].astype(f32) + got_cross.astype(f32)
+
+    def y_scatter(self, got_cross):
+        self.total = self.chip_sum(got_cross)
+        return [trade(cut(self.total, 1 - self.y, 2, self.y_axis).astype(bf16), 1, 8)]
+
+    def z_scatter(self, got):
+        self.half = cut(self.total, self.y, 2, self.y_axis) + got[0].astype(f32)
+        return [trade(cut(self.half, self.z ^ k, 4, self.z_axis).astype(bf16), 2 * k, 8) for k in (1, 2, 3)]
+
+    def z_gather(self, got):
+        mine = cut(self.half, self.z, 4, self.z_axis)
+        for part in got:
+            mine = mine + part.astype(f32)
+        self.mine = mine.astype(bf16)
+        return [trade(self.mine, 2 * k, 8) for k in (1, 2, 3)]
+
+    def y_gather(self, got):
+        self.parts = [self.mine, *got]
+        return [trade(jnp.concatenate(self.parts, axis=self.z_axis), 1, 8)]
+
+    def result(self, got):
+        far = [cut(got[0], k, 4, self.z_axis) for k in range(4)]
+        low = [jnp.where(self.y == 0, a, b) for a, b in zip(self.parts, far)]
+        high = [jnp.where(self.y == 0, b, a) for a, b in zip(self.parts, far)]
+        sides = [jnp.concatenate(ordered(side, self.z), axis=self.z_axis) for side in (low, high)]
+        return jnp.concatenate(sides, axis=self.y_axis).astype(f32)
 
 
 def masked_sums(pieces, masks, dtype):
@@ -448,40 +677,50 @@
     return total.astype(dtype)
 
 
-def exchange(own_states, positions, own, count, later):
-    local = own_states.shape[0]
-    table = positions.reshape(count, local)
-
-    def mask(target, sources):
-        there = table[target][:, None, None]
-        here = table[jnp.stack(sources)][None]
-        return ((here > there) if later else (here < there)).astype(f32)
-
-    pieces, sources = [own_states], [own]
-    for step in range(1, count // 2):
-        pieces.append(lax.ppermute(pieces[-1], "ctx", [(i, (i + 2) % count) for i in range(count)]))
-        sources.append((own - 2 * step) % count)
-    partner = own ^ 1
-    for_partner = masked_sums(pieces, mask(partner, sources), bf16)
-    received = lax.ppermute(for_partner, "ctx", [(i, i ^ 1) for i in range(count)])
-    return (masked_sums(pieces, mask(own, sources), f32) + received.astype(f32)).astype(bf16)
+class Exchange:
+    def __init__(self, states, positions, own, count, later):
+        self.pieces, self.sources, self.own, self.count, self.later = [states], [own], own, count, later
+        self.table = positions.reshape(count, states.shape[0])
+
+    def mask(self, target):
+        there = self.table[target][:, None, None]
+        here = self.table[jnp.stack(self.sources)][None]
+        return ((here > there) if self.later else (here < there)).astype(f32)
+
+    def ring(self):
+        return self.pieces[-1], "ctx", [(i, (i + 2) % self.count) for i in range(self.count)]
+
+    def masks(self):
+        self.sources = [(self.own - 2 * k) % self.count for k in range(self.count // 2)]
+        both = jnp.concatenate([self.mask(self.own), self.mask(self.own ^ 1)], axis=0)
+        return both.reshape(both.shape[0], -1)
+
+    def passed(self, piece):
+        self.sources.append((self.own - 2 * len(self.pieces)) % self.count)
+        self.pieces.append(piece)
+
+    def partner(self):
+        return trade(masked_sums(self.pieces, self.mask(self.own ^ 1), bf16), 1, self.count)
+
+    def total(self, received):
+        return (masked_sums(self.pieces, self.mask(self.own), f32) + received.astype(f32)).astype(bf16)
 
 
 def body(count):
     def layer(
         tokens, block_pos, gain_attn, w_query, w_key, w_value, w_out, gain_ffn, w_gate, w_up, w_down, cotangent
     ):
-        gather = lambda a: lax.all_gather(a, "fsdp", axis=0, tiled=True)
         own = lax.axis_index("ctx")
         me = lax.axis_index("fsdp").astype(jnp.int32).reshape(1)
         positions = block_pos[0]
-        gains = gather(jnp.stack([gain_attn, gain_ffn], axis=1)).astype(f32)
-        gain_one, gain_two = gains[:, 0], gains[:, 1]
-        in_full = gather(jnp.concatenate([w_query, w_key, w_value], axis=1))
-        gates = pieces(w_gate.T, in_full)
-        ups = pieces(w_up.T, in_full)
-        downs = pieces(w_down, gates[2])
-        out_full = gather(w_out)
+        in_shard = jnp.concatenate([w_query, w_key, w_value], axis=1)
+        gains = jnp.stack([gain_attn, gain_ffn])
+        if count == 8:
+            gains, in_full = gather_call(gains, in_shard)
+        else:
+            gains, in_full = (lax.all_gather(a, "fsdp") for a in (gains, in_shard))
+        gain_one, gain_two = (gains[:, k].reshape(-1).astype(f32) for k in (0, 1))
+        in_full = in_full.reshape(-1, in_shard.shape[1])
         residual = tokens[0].astype(f32)
         rows = residual.shape[0]
         inv_one = lax.rsqrt(jnp.mean(residual * residual, axis=-1, keepdims=True) + EPS)
@@ -494,10 +733,22 @@
         (own_states,) = attention_call(
             states_kernel, ("narrow", "wide"), (("state", bf16),), rows, unit * FEAT
         )(key, value)
-        numer, denom = attention_call(
-            intra_kernel, ("narrow", "narrow", "wide"), (("wide", f32), ("head", f32)), rows, unit * 256
-        )(query, key, value)
-        prefix = exchange(own_states, positions, own, count, False)
+        weights = (w_out, w_gate.T, w_up.T, w_down)
+        states = Exchange(own_states, positions, own, count, False)
+        if count == 8:
+            prefix, numer, denom, out_full, gates, ups, downs = forward_call(
+                states.masks(), own_states, query, key, value, weights
+            )
+        else:
+            numer, denom = attention_call(
+                intra_kernel, ("narrow", "narrow", "wide"), (("wide", f32), ("head", f32)), rows, unit * 256
+            )(query, key, value)
+            links = Links()
+            for _ in range(1, count // 2):
+                states.passed(links.round([states.ring()])[0])
+            prefix = states.total(links.round([states.partner()])[0])
+            out_full, gates, ups, downs = (lax.all_gather(w, "fsdp") for w in weights)
+        out_full = out_full.reshape(-1, w_out.shape[1])
         atten, denom = attention_call(
             inter_kernel, ("narrow", "state", "wide", "head"), (("wide", bf16), ("head", f32)), rows, unit * FEAT
         )(query, prefix, numer, denom)
@@ -522,35 +773,121 @@
             rows,
             unit * 512,
         )(query, key, value, gnumer, gdenom, prefix)
-        later = exchange(grad_states, positions, own, count, True)
-        gkey, gvalue = attention_call(
-            inter_back_kernel,
-            ("narrow", "wide", "state", "narrow", "wide"),
-            (("narrow", bf16), ("wide", bf16)),
-            rows,
-            unit * 256,
-        )(key, value, later, gkey, gvalue)
-        gprojected = jnp.concatenate([gquery, gkey, gvalue], axis=0)
-        gnormed_one = dot(gprojected, in_full, (0, 1))
-        weighted_one = gnormed_one * gain_one
-        grad_gain_one = jnp.sum(gnormed_one * residual * inv_one, axis=0)
-        grad_tokens = (
-            grad_middle
-            + inv_one * weighted_one
-            - residual * (inv_one * inv_one * inv_one) * jnp.mean(weighted_one * residual, axis=-1, keepdims=True)
-        )[None]
-        grad_gains = jnp.pad(jnp.stack([grad_gain_one, grad_gain_two[0]], axis=1), ((0, 0), (0, 126)))
-
         width = in_full.shape[1]
         out_keep, out_send = shard_grads(out_grad_kernel, me, atten, 0, [branch], [], branch.shape[1])
-        in_keep, in_send = shard_grads(
-            in_grad_kernel, me, normed_one, 1, [gquery, gkey, gvalue], [grad_gains], width + 128
-        )
-        down_grad = summed(down_keep, down_send, own, count, 1)
-        gate_grad = summed(gate_keep, gate_send, own, count, 0).T
-        up_grad = summed(up_keep, up_send, own, count, 0).T
-        out_grad = summed(out_keep, out_send, own, count, 0)
-        in_grad = summed(in_keep, in_send, own, count, 0)
+
+        def core(send):
+            return send, "fsdp", CORE
+
+        def ending(later, gkey, gvalue):
+            gkey, gvalue = attention_call(
+                inter_back_kernel,
+                ("narrow", "wide", "state", "narrow", "wide"),
+                (("narrow", bf16), ("wide", bf16)),
+                rows,
+                unit * 256,
+            )(key, value, later, gkey, gvalue)
+            gprojected = jnp.concatenate([gquery, gkey, gvalue], axis=0)
+            gnormed_one = dot(gprojected, in_full, (0, 1))
+            weighted_one = gnormed_one * gain_one
+            grad_gain_one = jnp.sum(gnormed_one * residual * inv_one, axis=0)
+            grad_tokens = (
+                grad_middle
+                + inv_one * weighted_one
+                - residual
+                * (inv_one * inv_one * inv_one)
+                * jnp.mean(weighted_one * residual, axis=-1, keepdims=True)
+            )[None]
+            grad_gains = jnp.pad(jnp.stack([grad_gain_one, grad_gain_two[0]], axis=1), ((0, 0), (0, 126)))
+            return grad_tokens, *shard_grads(
+                in_grad_kernel, me, normed_one, 1, [gquery, gkey, gvalue], [grad_gains], width + 128
+            )
+
+        backward = Exchange(grad_states, positions, own, count, True)
+        tall, wide = gate_keep.shape[1], down_keep.shape[1]
+        model = branch.shape[1]
+        links = Links()
+        if count == 8:
+            da, db = (Shard(down_keep, down_send, own, r, 1, 1) for r in ((0, wide // 2), (wide // 2, wide)))
+            ga, gb = (Shard(gate_keep, gate_send, own, r, 1, 0) for r in ((0, tall // 2), (tall // 2, tall)))
+            ua, ub = (Shard(up_keep, up_send, own, r, 1, 0) for r in ((0, tall // 2), (tall // 2, tall)))
+            o = Shard(out_keep, out_send, own, (0, model // 4), 1, 0)
+            (d_core,) = links.round([core(down_send)], (grad_states,))
+            piece, da_x, g_core = links.round(
+                [backward.ring(), da.cross(d_core), core(gate_send)], (gquery, gkey, gvalue)
+            )
+            backward.passed(piece)
+            piece, db_x, u_core, *da_y = links.round(
+                [backward.ring(), db.cross(d_core), core(up_send), *da.y_scatter(da_x)], (out_keep, out_send)
+            )
+            backward.passed(piece)
+            piece, ga_x, o_core, *db_y = links.round(
+                [backward.ring(), ga.cross(g_core), core(out_send), *db.y_scatter(db_x)]
+            )
+            backward.passed(piece)
+            got = links.round([backward.partner(), gb.cross(g_core), *da.z_scatter(da_y), *db.z_scatter(db_y)])
+            received, gb_x, da_z, db_z = got[0], got[1], got[2:5], got[5:8]
+            grad_tokens, in_keep, in_send = ending(backward.total(received), gkey, gvalue)
+            i = Shard(in_keep, in_send, own, (0, model // 4), 0, 0)
+            got = links.round(
+                [ua.cross(u_core), *ga.y_scatter(ga_x), *gb.y_scatter(gb_x), *da.z_gather(da_z), *db.z_gather(db_z)],
+                (in_keep, in_send),
+            )
+            ua_x, ga_y, gb_y, da_w, db_w = got[0], got[1:2], got[2:3], got[3:6], got[6:9]
+            got = links.round(
+                [
+                    ub.cross(u_core),
+                    core(in_send),
+                    *da.y_gather(da_w),
+                    *db.y_gather(db_w),
+                    *ga.z_scatter(ga_y),
+                    *gb.z_scatter(gb_y),
+                ]
+            )
+            ub_x, i_core, da_v, db_v, ga_z, gb_z = got[0], got[1], got[2:3], got[3:4], got[4:7], got[7:10]
+            got = links.round(
+                [i.cross(i_core), *ua.y_scatter(ua_x), *ub.y_scatter(ub_x), *ga.z_gather(ga_z), *gb.z_gather(gb_z)]
+            )
+            i_x, ua_y, ub_y, ga_w, gb_w = got[0], got[1:2], got[2:3], got[3:6], got[6:9]
+            got = links.round([o.cross(o_core), *i.y_scatter(i_x), *ua.z_scatter(ua_y), *ub.z_scatter(ub_y)])
+            o_x, i_y, ua_z, ub_z = got[0], got[1:2], got[2:5], got[5:8]
+            got = links.round(
+                [
+                    *o.y_scatter(o_x),
+                    *i.z_scatter(i_y),
+                    *ga.y_gather(ga_w),
+                    *gb.y_gather(gb_w),
+                    *ua.z_gather(ua_z),
+                    *ub.z_gather(ub_z),
+                ]
+            )
+            o_y, i_z, ga_v, gb_v, ua_w, ub_w = got[0:1], got[1:4], got[4:5], got[5:6], got[6:9], got[9:12]
+            got = links.round(
+                [*o.z_scatter(o_y), *i.z_gather(i_z), *ua.y_gather(ua_w), *ub.y_gather(ub_w)]
+            )
+            o_z, i_w, ua_v, ub_v = got[0:3], got[3:6], got[6:7], got[7:8]
+            got = links.round([*o.z_gather(o_z), *i.y_gather(i_w)])
+            o_w, i_v = got[0:3], got[3:4]
+            o_v = links.round(o.y_gather(o_w))
+            down_grad = jnp.concatenate([da.result(da_v), db.result(db_v)], axis=0)
+            gate_grad = jnp.concatenate([ga.result(ga_v), gb.result(gb_v)], axis=0).T
+            up_grad = jnp.concatenate([ua.result(ua_v), ub.result(ub_v)], axis=0).T
+            out_grad, in_grad = o.result(o_v), i.result(i_v)
+        else:
+            for _ in range(1, count // 2):
+                backward.passed(links.round([backward.ring()])[0])
+            grad_tokens, in_keep, in_send = ending(
+                backward.total(links.round([backward.partner()])[0]), gkey, gvalue
+            )
+
+            def summed(keep, send):
+                shard = Shard(keep, send, own, (0, keep.shape[1]), 0, 0)
+                (got,) = links.round([core(send)])
+                (got_cross,) = links.round([shard.cross(got)])
+                return lax.psum(shard.chip_sum(got_cross).astype(bf16), "ctx").astype(f32)
+
+            down_grad, gate_grad, up_grad = summed(down_keep, down_send), summed(gate_keep, gate_send).T, summed(up_keep, up_send).T
+            out_grad, in_grad = summed(out_keep, out_send), summed(in_keep, in_send)
         return (
             output[None],
             grad_tokens,

time: 601 us -> 490 us (0.82)
  waiting for transfers between devices: 340 us -> 99.5 us
  Pallas kernels: 78.5 us -> 192 us
  other arithmetic: 39.4 us -> 61.2 us
  between operations: 15.4 us -> 2.39 us
  starting transfers between devices: 89.6 us -> 98.4 us
  local copies, waits for them, and re-layouts: 11.5 us -> 17.9 us
    ppermute x67 -> x81, waiting for transfers between devices: 314 us -> 99.5 us  [round(): lax.ppermute(a, axis, perm)]
    pallas_call x0 -> x2, Pallas kernels: none -> 115 us  [the longest x1 90.2 us: forward_call(): pl.pallas_call(forward_kernel, out_shape=[jax.ShapeDtypeStruct(state, bf1...]
    all_gather x2 -> x0, waiting for transfers between devices: 25.3 us -> none  [layer(): gather = lambda a: lax.all_gather(a, 'fsdp', axis=0, tiled=True)]
    transpose x1 -> x2, other arithmetic: 2.93 us -> 25.2 us  [the longest x1 12.7 us: layer(): gate_grad = jnp.concatenate([ga.result(ga_v), gb.result(gb_v)], axis=0).T]
    ppermute x67 -> x81, starting transfers between devices: 89.5 us -> 98.4 us  [round(): lax.ppermute(a, axis, perm)]
    convert_element_type x17 -> x18, other arithmetic: 13.9 us -> 11.2 us  [the longest x5 8.07 us: cross(): (self.keep[1, start:stop].astype(f32) + got[1, start:stop].astype(f32)).a...]
    pallas_call x6 -> x5, Pallas kernels: 29.1 us -> 30 us  [call(): pl.pallas_call(kernel, out_shape=[jax.ShapeDtypeStruct(forms[name][2], dt...]
  transfers between devices with their start and end apart: 69 -> 81, of which waited for: 32 -> 33; matrix products, arithmetic and copies ran while one was open for 8% -> 13% of each run, Pallas kernels for 5% -> 6%
where the time goes in v2:
time: 490 us; the launch traced here: 481 us
  Pallas kernels  192 us (39%)
  waiting for transfers between devices  99.5 us (20%)
  starting transfers between devices  98.4 us (20%)
  other arithmetic  61.2 us (12%)
  local copies, waits for them, and re-layouts  17.9 us (4%)
  matrix products  10.5 us (2%)
    ppermute x81, waiting for transfers between devices, round(): lax.ppermute(a, axis, perm)  99.5 us
    ppermute x81, starting transfers between devices, round(): lax.ppermute(a, axis, perm)  98.4 us
    pallas_call x1, Pallas kernels, forward_call(): pl.pallas_call(forward_kernel, out_shape=[jax.ShapeDtypeStruct(state, bf1...  90.2 us
    pallas_call x1, Pallas kernels, ffn_call(): pl.pallas_call(ffn_kernel, out_shape=[jax.ShapeDtypeStruct((rows, model),...  41.5 us
    pallas_call x5, Pallas kernels, call(): pl.pallas_call(kernel, out_shape=[jax.ShapeDtypeStruct(forms[name][2], dt...  30 us
    pallas_call x1, Pallas kernels, gather_call(): pl.pallas_call(gather_kernel, out_shape=[jax.ShapeDtypeStruct((4, *a.shap...  24.6 us
    transpose x1, other arithmetic, layer(): gate_grad = jnp.concatenate([ga.result(ga_v), gb.result(gb_v)], axis=0).T  12.7 us
    transpose x1, other arithmetic, layer(): up_grad = jnp.concatenate([ua.result(ua_v), ub.result(ub_v)], axis=0).T  12.5 us
  transfers between devices with their start and end apart: 81, of which 33 were waited for; matrix products, arithmetic and copies ran while one was open for 13% of the time, Pallas kernels for 6%

profile of v2, /device:TPU:0, one launch (start us, length us, event | category | flops | bytes accessed | tf_op | source)
XLA Modules:
  0.0 481.3 jit_solution(16439166551894855646)
XLA Ops:
  3.3 24.6 %shard_map.203 = (bf16[4,2,256]{2,1,0:T(2,128)(2,1)S(1)}, bf16[4,256,1536]{2,1,0:T(8,128)(2,1)S(1)}) custom-call(bf16[2,256]{1,0:T(2,128)(2,1)S(1)} %pad_maximum_fusion.10.gain_ref, bf16[256,1536]{1,0:T(8,128)(2,1)S(1)} %pad_maximum_fusion.in_ref), custom_call_target="tpu_custom_call" | custom-call | tf_op jit(solution)/shard_map/pallas_call | solution.py:594
  39.3 90.2 %shard_map.205 = (bf16[2,2,656,128]{3,2,1,0:T(8,128)(2,1)S(1)}, f32[1024,512]{1,0:T(8,128)S(1)}, f32[16,512]{1,0:T(8,128)S(1)}, bf16[4,256,1024]{2,1,0:T(8,128)(...) custom-call(f32[4,8]{1,0:T(4,128)S(1)} %add_convert_fusion.18.mask_ref, ...), custom_call_target="tpu_custom_call" | custom-call | tf_op jit(solution)/shard_map/pallas_call | solution.py:607
  129.5 2.6 shard_map.206
  132.1 2.6 fusion.4.middle_ref
  134.7 41.5 %shard_map.207 = (bf16[512,1024]{1,0:T(8,128)(2,1)}, f32[512,1024]{1,0:T(8,128)}, bf16[512,1024]{1,0:T(8,128)(2,1)}, f32[8,1024]{1,0:T(8,128)}, bf16[2,2752,256]...) custom-call(s32[1]{0:T(128)} %bitcast.me_ref, ...), custom_call_target="tpu_custom_call" | custom-call | flops 25971130368 | bytes 39452672 | tf_op jit(solution)/shard_map/pallas_call | solution.py:276
  176.7 2.5 fusion.49.grad_ref
  179.2 2.4 shard_map.208
  188.0 19.5 %shard_map.209 = (bf16[256,512]{1,0:T(8,128)(2,1)S(1)}, f32[256,512]{1,0:T(8,128)S(1)}, f32[1024,512]{1,0:T(8,128)S(1)}) custom-call(bf16[256,512]{1,0:T(8,128)(2,1)S(1)} %get-tuple-element.332.query_ref, bf16[256,512]{1,0:T(8,128)(2,1)S(1)} %get-tuple-element.331.key_ref, bf16[1024,512]{1,0:T(8,128)(2,1)S(1)} %slice.282.value_ref, ...), custom_call_target="tpu_custom_call" | custom-call | flops 2147483648 | bytes 6651904 | tf_op jit(solution)/shard_map/pallas_call | solution.py:177
  207.6 2.9 bitcast_add_fusion.6
  221.2 2.7 fusion.31
  223.9 5.8 %collective-permute-done.7 = bf16[344,512]{1,0:T(8,128)(2,1)S(1)} collective-permute-done((bf16[344,512]{1,0:T(8,128)(2,1)S(1)}, bf16[344,512]{1,0:T(8,128)(2,1)S(1)}, u32[]{:S(2)}, u32[]{:S(2)}) %collective-permute-start.7) | collective-permute-done | bytes 352288 | tf_op jit(solution)/shard_map/ppermute | solution.py:398
  229.8 6.3 %collective-permute-done.5 = bf16[344,1024]{1,0:T(8,128)(2,1)S(1)} collective-permute-done((bf16[344,1024]{1,0:T(8,128)(2,1)S(1)}, bf16[344,1024]{1,0:T(8,128)(2,1)S(1)}, u32[]{:S(2)}, u32[]{:S(2)}) %collective-permute-start.5) | collective-permute-done | bytes 704544 | tf_op jit(solution)/shard_map/ppermute | solution.py:398
  241.4 6.3 %collective-permute-done.9 = bf16[344,512]{1,0:T(8,128)(2,1)S(1)} collective-permute-done((bf16[344,512]{1,0:T(8,128)(2,1)S(1)}, bf16[344,512]{1,0:T(8,128)(2,1)S(1)}, u32[]{:S(2)}, u32[]{:S(2)}) %collective-permute-start.9) | collective-permute-done | bytes 352288 | tf_op jit(solution)/shard_map/ppermute | solution.py:398
  247.9 9.9 %collective-permute-done.8 = bf16[2,2,656,128]{3,2,1,0:T(8,128)(2,1)S(1)} collective-permute-done((bf16[2,2,656,128]{3,2,1,0:T(8,128)(2,1)S(1)}, bf16[2,2,656,128]{3,2,1,0:T(8,128)(2,1)S(1)}, u32[]{:S(2)}, u32[]{:S(2)}) %collective-permute-start.8) | collective-permute-done | bytes 671776 | tf_op jit(solution)/shard_map/ppermute | solution.py:398
  259.7 2.8 collective-permute-start.18
  264.4 2.8 fusion.33
  267.8 2.4 collective-permute-start.14
  273.6 3.7 collective-permute-done.14
  277.4 2.6 collective-permute-done.12
  281.6 3.3 shard_map.211
  285.0 3.4 fusion.14
  288.8 4.4 fusion.12
  296.7 2.4 collective-permute-start.24
  300.6 3.2 shard_map.212
  305.3 3.0 collective-permute-start.21
  312.1 2.5 collective-permute-done.22
  315.0 10.0 %collective-permute-done.28 = bf16[1376,256]{1,0:T(8,128)(2,1)S(1)} collective-permute-done((bf16[1376,256]{1,0:T(8,128)(2,1)S(1)}, bf16[1376,256]{1,0:T(8,128)(2,1)S(1)}, u32[]{:S(2)}, u32[]{:S(2)}) %collective-permute-start.28) | collective-permute-done | bytes 704544 | tf_op jit(solution)/shard_map/ppermute | solution.py:398
  326.6 2.8 collective-permute-start.36
  331.7 3.4 collective-permute-done.35
  337.8 2.7 collective-permute-done.32
  343.0 5.1 %collective-permute-done.30 = bf16[1376,256]{1,0:T(8,128)(2,1)S(1)} collective-permute-done((bf16[1376,256]{1,0:T(8,128)(2,1)S(1)}, bf16[1376,256]{1,0:T(8,128)(2,1)S(1)}, u32[]{:S(2)}, u32[]{:S(2)}) %collective-permute-start.30) | collective-permute-done | bytes 704544 | tf_op jit(solution)/shard_map/ppermute | solution.py:398
  358.6 4.7 collective-permute-done.46
  363.3 2.3 collective-permute-start.43
  365.7 2.6 collective-permute-start.44
  368.5 3.5 collective-permute-done.39
  373.3 2.8 collective-permute-start.54
  377.7 2.8 collective-permute-start.51
  386.9 3.3 collective-permute-done.49
  393.1 2.6 collective-permute-start.64
  398.7 3.3 collective-permute-start.61
  413.5 2.5 collective-permute-done.59
  416.2 5.3 %collective-permute-done.66 = bf16[1376,128]{1,0:T(8,128)(2,1)S(1)} collective-permute-done((bf16[1376,128]{1,0:T(8,128)(2,1)S(1)}, bf16[1376,128]{1,0:T(8,128)(2,1)S(1)}, u32[]{:S(2)}, u32[]{:S(2)}) %collective-permute-start.66) | collective-permute-done | bytes 352288 | tf_op jit(solution)/shard_map/ppermute | solution.py:398
  421.5 4.7 collective-permute-done.67
  429.9 2.6 collective-permute-start.71
  433.3 12.7 %convert_bitcast_fusion.1 = f32[256,2752]{0,1:T(8,128)} fusion(bf16[344,128]{1,0:T(8,128)(2,1)S(1)} %get-tuple-element.417, bf16[344,128]{1,0:T(8,128)(2,1)S(1)} %get-tuple-element.416, bf16[344,128]{1,0:T(8,128)(2,1)S(1)} %get-tuple-element.415, bf16[344,128]{1,0:T(8,128)(2,1)S(1)} %get-tuple-element.355, bf16[344,128]{1,0:T(8,128)(2,1)S(1)} %get-tuple-element.414, ...), kind=kLoop, calls=%fused_computation.4 | loop fusion | flops 22544384 | bytes 4227072 | tf_op jit(solution)/shard_map/transpose | solution.py:873
  447.3 3.2 collective-permute-start.73
  450.5 2.2 collective-permute-done.68
  460.7 12.5 %convert_bitcast_fusion = f32[256,2752]{0,1:T(8,128)} fusion(bf16[344,128]{1,0:T(8,128)(2,1)S(1)} %get-tuple-element.405, bf16[344,128]{1,0:T(8,128)(2,1)S(1)} %get-tuple-element.404, bf16[344,128]{1,0:T(8,128)(2,1)S(1)} %get-tuple-element.403, bf16[344,128]{1,0:T(8,128)(2,1)S(1)} %get-tuple-element.345, bf16[344,128]{1,0:T(8,128)(2,1)S(1)} %get-tuple-element.402, ...), kind=kLoop, calls=%fused_computation.3 | loop fusion | flops 22544384 | bytes 4227072 | tf_op jit(solution)/shard_map/transpose | solution.py:874
  (343 shorter events, 124.8 us)
Async XLA Ops:
  184.1 27.5 %collective-permute-start.3 = (bf16[2,2752,256]{2,1,0:T(8,128)(2,1)}, bf16[2,2752,256]{2,1,0:T(8,128)(2,1)}, u32[]{:S(2)}, u32[]{:S(2)}) collective-permute-start(bf16[2,2752,256]{2,1,0:T(8,128)(2,1)} %get-tuple-element.148), channel_id=1, source_target_pairs={{0,1},{1,0},{2,3},{3,2},{4,5},{5,4},{6,7},{7,6},{8,9},{9,8},{10,11... | collective-permute-start | bytes 8454152 | tf_op jit(solution)/shard_map/ppermute | solution.py:398
  184.1 23.4 %collective-permute-start.2 = (bf16[344,1024]{1,0:T(8,128)(2,1)}, bf16[344,1024]{1,0:T(8,128)(2,1)}, u32[]{:S(2)}, u32[]{:S(2)}) collective-permute-start(bf16[344,1024]{1,0:T(8,128)(2,1)} %get-tuple-element.147), channel_id=1, source_target_pairs={{0,2},{2,0},{1,3},{3,1},{4,6},{6,4},{5,7},{7,5},{8,10},{10,8},{9,1... | collective-permute-start | bytes 2113544 | tf_op jit(solution)/shard_map/ppermute | solution.py:398
  185.6 24.9 %collective-permute-start.1 = (bf16[2,2,656,128]{3,2,1,0:T(8,128)(2,1)S(1)}, bf16[2,2,656,128]{3,2,1,0:T(8,128)(2,1)}, u32[]{:S(2)}, u32[]{:S(2)}) collective-permute-start(bf16[2,2,656,128]{3,2,1,0:T(8,128)(2,1)S(1)} %get-tuple-element.145), channel_id=1, source_target_pairs={{0,8},{4,12},{8,16},{12,20},{16,24},{20,28},{24,0},{28,4},{1,9},{5... | collective-permute-start | bytes 2015240 | tf_op jit(solution)/shard_map/ppermute | solution.py:398
  211.6 26.4 %collective-permute-start.6 = (bf16[2,2752,256]{2,1,0:T(8,128)(2,1)}, bf16[2,2752,256]{2,1,0:T(8,128)(2,1)}, u32[]{:S(2)}, u32[]{:S(2)}) collective-permute-start(bf16[2,2752,256]{2,1,0:T(8,128)(2,1)} %get-tuple-element.155), channel_id=1, source_target_pairs={{0,1},{1,0},{2,3},{3,2},{4,5},{5,4},{6,7},{7,6},{8,9},{9,8},{10,11... | collective-permute-start | bytes 8454152 | tf_op jit(solution)/shard_map/ppermute | solution.py:398
  218.0 18.1 %collective-permute-start.5 = (bf16[344,1024]{1,0:T(8,128)(2,1)S(1)}, bf16[344,1024]{1,0:T(8,128)(2,1)S(1)}, u32[]{:S(2)}, u32[]{:S(2)}) collective-permute-start(bf16[344,1024]{1,0:T(8,128)(2,1)S(1)} %copy-done.37), channel_id=1, source_target_pairs={{0,2},{2,0},{1,3},{3,1},{4,6},{6,4},{5,7},{7,5},{8,10},{10,8},{9,1... | collective-permute-start | bytes 2113544 | tf_op jit(solution)/shard_map/ppermute | solution.py:398
  218.6 19.3 %collective-permute-start.4 = (bf16[2,2,656,128]{3,2,1,0:T(8,128)(2,1)}, bf16[2,2,656,128]{3,2,1,0:T(8,128)(2,1)S(1)}, u32[]{:S(2)}, u32[]{:S(2)}) collective-permute-start(bf16[2,2,656,128]{3,2,1,0:T(8,128)(2,1)} %collective-permute-done.1), channel_id=1, source_target_pairs={{0,8},{4,12},{8,16},{12,20},{16,24},{20,28},{24,0},{28,4},{1,9},{5... | collective-permute-start | bytes 2015240 | tf_op jit(solution)/shard_map/ppermute | solution.py:398
  219.7 10.0 %collective-permute-start.7 = (bf16[344,512]{1,0:T(8,128)(2,1)S(1)}, bf16[344,512]{1,0:T(8,128)(2,1)S(1)}, u32[]{:S(2)}, u32[]{:S(2)}) collective-permute-start(bf16[344,512]{1,0:T(8,128)(2,1)S(1)} %dynamic-slice_convert_fusion.6), channel_id=1, source_target_pairs={{0,4},{4,0},{8,12},{12,8},{16,20},{20,16},{24,28},{28,24},{1,5},{5... | collective-permute-start | bytes 1056776 | tf_op jit(solution)/shard_map/ppermute | solution.py:398
  238.0 9.7 %collective-permute-start.9 = (bf16[344,512]{1,0:T(8,128)(2,1)S(1)}, bf16[344,512]{1,0:T(8,128)(2,1)S(1)}, u32[]{:S(2)}, u32[]{:S(2)}) collective-permute-start(bf16[344,512]{1,0:T(8,128)(2,1)S(1)} %dynamic-slice_convert_fusion.5), channel_id=1, source_target_pairs={{0,4},{4,0},{8,12},{12,8},{16,20},{20,16},{24,28},{28,24},{1,5},{5... | collective-permute-start | bytes 1056776 | tf_op jit(solution)/shard_map/ppermute | solution.py:398
  239.5 18.3 %collective-permute-start.8 = (bf16[2,2,656,128]{3,2,1,0:T(8,128)(2,1)S(1)}, bf16[2,2,656,128]{3,2,1,0:T(8,128)(2,1)S(1)}, u32[]{:S(2)}, u32[]{:S(2)}) collective-permute-start(bf16[2,2,656,128]{3,2,1,0:T(8,128)(2,1)S(1)} %collective-permute-done.4), channel_id=1, source_target_pairs={{0,8},{4,12},{8,16},{12,20},{16,24},{20,28},{24,0},{28,4},{1,9},{5... | collective-permute-start | bytes 2015240 | tf_op jit(solution)/shard_map/ppermute | solution.py:398
  240.6 18.4 %collective-permute-start.11 = (bf16[2,256,1024]{2,1,0:T(8,128)(2,1)S(1)}, bf16[2,256,1024]{2,1,0:T(8,128)(2,1)S(1)}, u32[]{:S(2)}, u32[]{:S(2)}) collective-permute-start(bf16[2,256,1024]{2,1,0:T(8,128)(2,1)S(1)} %get-tuple-element.161), channel_id=1, source_target_pairs={{0,1},{1,0},{2,3},{3,2},{4,5},{5,4},{6,7},{7,6},{8,9},{9,8},{10,11... | collective-permute-start | bytes 3145736 | tf_op jit(solution)/shard_map/ppermute | solution.py:398
  240.8 18.2 %collective-permute-start.10 = (bf16[1376,256]{1,0:T(8,128)(2,1)S(1)}, bf16[1376,256]{1,0:T(8,128)(2,1)S(1)}, u32[]{:S(2)}, u32[]{:S(2)}) collective-permute-start(bf16[1376,256]{1,0:T(8,128)(2,1)S(1)} %get-tuple-element.160), channel_id=1, source_target_pairs={{0,2},{2,0},{1,3},{3,1},{4,6},{6,4},{5,7},{7,5},{8,10},{10,8},{9,1... | collective-permute-start | bytes 2113544 | tf_op jit(solution)/shard_map/ppermute | solution.py:398
  259.7 10.6 %collective-permute-start.18 = (bf16[344,128]{1,0:T(8,128)(2,1)S(1)}, bf16[344,128]{1,0:T(8,128)(2,1)S(1)}, u32[]{:S(2)}, u32[]{:S(2)}) collective-permute-start(bf16[344,128]{1,0:T(8,128)(2,1)S(1)} %get-tuple-element.174), channel_id=1, source_target_pairs={{0,16},{4,20},{8,24},{12,28},{16,0},{20,4},{24,8},{28,12},{1,17},{... | collective-permute-start | bytes 264200 | tf_op jit(solution)/shard_map/ppermute | solution.py:398
  262.5 9.9 %collective-permute-start.19 = (bf16[344,128]{1,0:T(8,128)(2,1)S(1)}, bf16[344,128]{1,0:T(8,128)(2,1)S(1)}, u32[]{:S(2)}, u32[]{:S(2)}) collective-permute-start(bf16[344,128]{1,0:T(8,128)(2,1)S(1)} %get-tuple-element.175), channel_id=1, source_target_pairs={{0,24},{4,28},{8,16},{12,20},{16,8},{20,12},{24,0},{28,4},{1,25},{... | collective-permute-start | bytes 264200 | tf_op jit(solution)/shard_map/ppermute | solution.py:398
  263.8 16.1 %collective-permute-start.12 = (bf16[2,2,656,128]{3,2,1,0:T(8,128)(2,1)S(1)}, bf16[2,2,656,128]{3,2,1,0:T(8,128)(2,1)S(1)}, u32[]{:S(2)}, u32[]{:S(2)}) collective-permute-start(bf16[2,2,656,128]{3,2,1,0:T(8,128)(2,1)S(1)} %add_convert_fusion.8), channel_id=1, source_target_pairs={{0,4},{4,0},{8,12},{12,8},{16,20},{20,16},{24,28},{28,24},{1,5},{5... | collective-permute-start | bytes 2015240 | tf_op jit(solution)/shard_map/ppermute | solution.py:398
  267.8 9.5 %collective-permute-start.14 = (bf16[344,128]{1,0:T(8,128)(2,1)S(1)}, bf16[344,128]{1,0:T(8,128)(2,1)S(1)}, u32[]{:S(2)}, u32[]{:S(2)}) collective-permute-start(bf16[344,128]{1,0:T(8,128)(2,1)S(1)} %get-tuple-element.170), channel_id=1, source_target_pairs={{0,16},{4,20},{8,24},{12,28},{16,0},{20,4},{24,8},{28,12},{1,17},{... | collective-permute-start | bytes 264200 | tf_op jit(solution)/shard_map/ppermute | solution.py:398
  272.3 20.8 %collective-permute-start.16 = (bf16[1376,256]{1,0:T(8,128)(2,1)}, bf16[1376,256]{1,0:T(8,128)(2,1)}, u32[]{:S(2)}, u32[]{:S(2)}) collective-permute-start(bf16[1376,256]{1,0:T(8,128)(2,1)} %get-tuple-element.172), channel_id=1, source_target_pairs={{0,2},{2,0},{1,3},{3,1},{4,6},{6,4},{5,7},{7,5},{8,10},{10,8},{9,1... | collective-permute-start | bytes 2113544 | tf_op jit(solution)/shard_map/ppermute | solution.py:398
  295.5 19.2 %collective-permute-start.27 = (bf16[1376,128]{1,0:T(8,128)(2,1)S(1)}, bf16[1376,128]{1,0:T(8,128)(2,1)S(1)}, u32[]{:S(2)}, u32[]{:S(2)}) collective-permute-start(bf16[1376,128]{1,0:T(8,128)(2,1)S(1)} %dynamic-slice_convert_fusion.3), channel_id=1, source_target_pairs={{0,4},{4,0},{8,12},{12,8},{16,20},{20,16},{24,28},{28,24},{1,5},{5... | collective-permute-start | bytes 1056776 | tf_op jit(solution)/shard_map/ppermute | solution.py:398
  296.2 9.1 %collective-permute-start.23 = (bf16[344,128]{1,0:T(8,128)(2,1)S(1)}, bf16[344,128]{1,0:T(8,128)(2,1)S(1)}, u32[]{:S(2)}, u32[]{:S(2)}) collective-permute-start(bf16[344,128]{1,0:T(8,128)(2,1)S(1)} %add_convert_fusion.15), channel_id=1, source_target_pairs={{0,8},{4,12},{8,0},{12,4},{16,24},{20,28},{24,16},{28,20},{1,9},{5... | collective-permute-start | bytes 264200 | tf_op jit(solution)/shard_map/ppermute | solution.py:398
  299.2 9.1 %collective-permute-start.25 = (bf16[344,128]{1,0:T(8,128)(2,1)S(1)}, bf16[344,128]{1,0:T(8,128)(2,1)S(1)}, u32[]{:S(2)}, u32[]{:S(2)}) collective-permute-start(bf16[344,128]{1,0:T(8,128)(2,1)S(1)} %add_convert_fusion.15), channel_id=1, source_target_pairs={{0,24},{4,28},{8,16},{12,20},{16,8},{20,12},{24,0},{28,4},{1,25},{... | collective-permute-start | bytes 264200 | tf_op jit(solution)/shard_map/ppermute | solution.py:398
  303.8 11.0 %collective-permute-start.26 = (bf16[1376,128]{1,0:T(8,128)(2,1)S(1)}, bf16[1376,128]{1,0:T(8,128)(2,1)S(1)}, u32[]{:S(2)}, u32[]{:S(2)}) collective-permute-start(bf16[1376,128]{1,0:T(8,128)(2,1)S(1)} %dynamic-slice_convert_fusion.4), channel_id=1, source_target_pairs={{0,4},{4,0},{8,12},{12,8},{16,20},{20,16},{24,28},{28,24},{1,5},{5... | collective-permute-start | bytes 1056776 | tf_op jit(solution)/shard_map/ppermute | solution.py:398
  311.7 13.3 %collective-permute-start.28 = (bf16[1376,256]{1,0:T(8,128)(2,1)S(1)}, bf16[1376,256]{1,0:T(8,128)(2,1)S(1)}, u32[]{:S(2)}, u32[]{:S(2)}) collective-permute-start(bf16[1376,256]{1,0:T(8,128)(2,1)S(1)} %copy-done.38), channel_id=1, source_target_pairs={{0,2},{2,0},{1,3},{3,1},{4,6},{6,4},{5,7},{7,5},{8,10},{10,8},{9,1... | collective-permute-start | bytes 2113544 | tf_op jit(solution)/shard_map/ppermute | solution.py:398
  325.0 10.1 %collective-permute-start.35 = (bf16[344,128]{1,0:T(8,128)(2,1)S(1)}, bf16[344,128]{1,0:T(8,128)(2,1)S(1)}, u32[]{:S(2)}, u32[]{:S(2)}) collective-permute-start(bf16[344,128]{1,0:T(8,128)(2,1)S(1)} %get-tuple-element.191), channel_id=1, source_target_pairs={{0,16},{4,20},{8,24},{12,28},{16,0},{20,4},{24,8},{28,12},{1,17},{... | collective-permute-start | bytes 264200 | tf_op jit(solution)/shard_map/ppermute | solution.py:398
  329.6 12.0 %collective-permute-start.37 = (bf16[344,512]{1,0:T(8,128)(2,1)S(1)}, bf16[344,512]{1,0:T(8,128)(2,1)S(1)}, u32[]{:S(2)}, u32[]{:S(2)}) collective-permute-start(bf16[344,512]{1,0:T(8,128)(2,1)S(1)} %pad_maximum_fusion.2), channel_id=1, source_target_pairs={{0,4},{4,0},{8,12},{12,8},{16,20},{20,16},{24,28},{28,24},{1,5},{5... | collective-permute-start | bytes 1056776 | tf_op jit(solution)/shard_map/ppermute | solution.py:398
  330.3 12.0 %collective-permute-start.38 = (bf16[344,512]{1,0:T(8,128)(2,1)S(1)}, bf16[344,512]{1,0:T(8,128)(2,1)S(1)}, u32[]{:S(2)}, u32[]{:S(2)}) collective-permute-start(bf16[344,512]{1,0:T(8,128)(2,1)S(1)} %pad_maximum_fusion.3), channel_id=1, source_target_pairs={{0,4},{4,0},{8,12},{12,8},{16,20},{20,16},{24,28},{28,24},{1,5},{5... | collective-permute-start | bytes 1056776 | tf_op jit(solution)/shard_map/ppermute | solution.py:398
  336.8 11.2 %collective-permute-start.30 = (bf16[1376,256]{1,0:T(8,128)(2,1)S(1)}, bf16[1376,256]{1,0:T(8,128)(2,1)S(1)}, u32[]{:S(2)}, u32[]{:S(2)}) collective-permute-start(bf16[1376,256]{1,0:T(8,128)(2,1)S(1)} %copy-done.36), channel_id=1, source_target_pairs={{0,2},{2,0},{1,3},{3,1},{4,6},{6,4},{5,7},{7,5},{8,10},{10,8},{9,1... | collective-permute-start | bytes 2113544 | tf_op jit(solution)/shard_map/ppermute | solution.py:398
  340.5 9.5 %collective-permute-start.29 = (bf16[2,256,1664]{2,1,0:T(8,128)(2,1)S(1)}, bf16[2,256,1664]{2,1,0:T(8,128)(2,1)S(1)}, u32[]{:S(2)}, u32[]{:S(2)}) collective-permute-start(bf16[2,256,1664]{2,1,0:T(8,128)(2,1)S(1)} %get-tuple-element.185), channel_id=1, source_target_pairs={{0,1},{1,0},{2,3},{3,2},{4,5},{5,4},{6,7},{7,6},{8,9},{9,8},{10,11... | collective-permute-start | bytes 5111816 | tf_op jit(solution)/shard_map/ppermute | solution.py:398
  350.2 15.4 %collective-permute-start.41 = (bf16[1376,128]{1,0:T(8,128)(2,1)S(1)}, bf16[1376,128]{1,0:T(8,128)(2,1)S(1)}, u32[]{:S(2)}, u32[]{:S(2)}) collective-permute-start(bf16[1376,128]{1,0:T(8,128)(2,1)S(1)} %dynamic-slice_convert_fusion.1), channel_id=1, source_target_pairs={{0,4},{4,0},{8,12},{12,8},{16,20},{20,16},{24,28},{28,24},{1,5},{5... | collective-permute-start | bytes 1056776 | tf_op jit(solution)/shard_map/ppermute | solution.py:398
  353.6 9.7 %collective-permute-start.46 = (bf16[344,128]{1,0:T(8,128)(2,1)S(1)}, bf16[344,128]{1,0:T(8,128)(2,1)S(1)}, u32[]{:S(2)}, u32[]{:S(2)}) collective-permute-start(bf16[344,128]{1,0:T(8,128)(2,1)S(1)} %add_convert_fusion.13), channel_id=1, source_target_pairs={{0,16},{4,20},{8,24},{12,28},{16,0},{20,4},{24,8},{28,12},{1,17},{... | collective-permute-start | bytes 264200 | tf_op jit(solution)/shard_map/ppermute | solution.py:398
  356.0 12.3 %collective-permute-start.40 = (bf16[1376,128]{1,0:T(8,128)(2,1)S(1)}, bf16[1376,128]{1,0:T(8,128)(2,1)S(1)}, u32[]{:S(2)}, u32[]{:S(2)}) collective-permute-start(bf16[1376,128]{1,0:T(8,128)(2,1)S(1)} %dynamic-slice_convert_fusion.2), channel_id=1, source_target_pairs={{0,4},{4,0},{8,12},{12,8},{16,20},{20,16},{24,28},{28,24},{1,5},{5... | collective-permute-start | bytes 1056776 | tf_op jit(solution)/shard_map/ppermute | solution.py:398
  357.1 14.8 %collective-permute-start.39 = (bf16[256,1664]{1,0:T(8,128)(2,1)S(1)}, bf16[256,1664]{1,0:T(8,128)(2,1)S(1)}, u32[]{:S(2)}, u32[]{:S(2)}) collective-permute-start(bf16[256,1664]{1,0:T(8,128)(2,1)S(1)} %fusion.27), channel_id=1, source_target_pairs={{0,2},{2,0},{1,3},{3,1},{4,6},{6,4},{5,7},{7,5},{8,10},{10,8},{9,1... | collective-permute-start | bytes 2555912 | tf_op jit(solution)/shard_map/ppermute | solution.py:398
  363.3 9.0 %collective-permute-start.43 = (bf16[344,128]{1,0:T(8,128)(2,1)S(1)}, bf16[344,128]{1,0:T(8,128)(2,1)S(1)}, u32[]{:S(2)}, u32[]{:S(2)}) collective-permute-start(bf16[344,128]{1,0:T(8,128)(2,1)S(1)} %add_convert_fusion.14), channel_id=1, source_target_pairs={{0,16},{4,20},{8,24},{12,28},{16,0},{20,4},{24,8},{28,12},{1,17},{... | collective-permute-start | bytes 264200 | tf_op jit(solution)/shard_map/ppermute | solution.py:398
  382.8 9.2 %collective-permute-start.48 = (bf16[256,1024]{1,0:T(8,128)(2,1)S(1)}, bf16[256,1024]{1,0:T(8,128)(2,1)S(1)}, u32[]{:S(2)}, u32[]{:S(2)}) collective-permute-start(bf16[256,1024]{1,0:T(8,128)(2,1)S(1)} %fusion.34), channel_id=1, source_target_pairs={{0,2},{2,0},{1,3},{3,1},{4,6},{6,4},{5,7},{7,5},{8,10},{10,8},{9,1... | collective-permute-start | bytes 1572872 | tf_op jit(solution)/shard_map/ppermute | solution.py:398
  392.3 9.7 %collective-permute-start.63 = (bf16[344,128]{1,0:T(8,128)(2,1)S(1)}, bf16[344,128]{1,0:T(8,128)(2,1)S(1)}, u32[]{:S(2)}, u32[]{:S(2)}) collective-permute-start(bf16[344,128]{1,0:T(8,128)(2,1)S(1)} %add_convert_fusion.11), channel_id=1, source_target_pairs={{0,8},{4,12},{8,0},{12,4},{16,24},{20,28},{24,16},{28,20},{1,9},{5... | collective-permute-start | bytes 264200 | tf_op jit(solution)/shard_map/ppermute | solution.py:398
  393.1 10.5 %collective-permute-start.64 = (bf16[344,128]{1,0:T(8,128)(2,1)S(1)}, bf16[344,128]{1,0:T(8,128)(2,1)S(1)}, u32[]{:S(2)}, u32[]{:S(2)}) collective-permute-start(bf16[344,128]{1,0:T(8,128)(2,1)S(1)} %add_convert_fusion.11), channel_id=1, source_target_pairs={{0,16},{4,20},{8,24},{12,28},{16,0},{20,4},{24,8},{28,12},{1,17},{... | collective-permute-start | bytes 264200 | tf_op jit(solution)/shard_map/ppermute | solution.py:398
  395.7 9.2 %collective-permute-start.65 = (bf16[344,128]{1,0:T(8,128)(2,1)S(1)}, bf16[344,128]{1,0:T(8,128)(2,1)S(1)}, u32[]{:S(2)}, u32[]{:S(2)}) collective-permute-start(bf16[344,128]{1,0:T(8,128)(2,1)S(1)} %add_convert_fusion.11), channel_id=1, source_target_pairs={{0,24},{4,28},{8,16},{12,20},{16,8},{20,12},{24,0},{28,4},{1,25},{... | collective-permute-start | bytes 264200 | tf_op jit(solution)/shard_map/ppermute | solution.py:398
  398.7 9.9 %collective-permute-start.61 = (bf16[344,128]{1,0:T(8,128)(2,1)S(1)}, bf16[344,128]{1,0:T(8,128)(2,1)S(1)}, u32[]{:S(2)}, u32[]{:S(2)}) collective-permute-start(bf16[344,128]{1,0:T(8,128)(2,1)S(1)} %add_convert_fusion.12), channel_id=1, source_target_pairs={{0,16},{4,20},{8,24},{12,28},{16,0},{20,4},{24,8},{28,12},{1,17},{... | collective-permute-start | bytes 264200 | tf_op jit(solution)/shard_map/ppermute | solution.py:398
  403.6 12.5 %collective-permute-start.56 = (bf16[256,512]{1,0:T(8,128)(2,1)S(1)}, bf16[256,512]{1,0:T(8,128)(2,1)S(1)}, u32[]{:S(2)}, u32[]{:S(2)}) collective-permute-start(bf16[256,512]{1,0:T(8,128)(2,1)S(1)} %dynamic-slice_convert_fusion.7), channel_id=1, source_target_pairs={{0,4},{4,0},{8,12},{12,8},{16,20},{20,16},{24,28},{28,24},{1,5},{5... | collective-permute-start | bytes 786440 | tf_op jit(solution)/shard_map/ppermute | solution.py:398
  410.3 11.2 %collective-permute-start.66 = (bf16[1376,128]{1,0:T(8,128)(2,1)S(1)}, bf16[1376,128]{1,0:T(8,128)(2,1)S(1)}, u32[]{:S(2)}, u32[]{:S(2)}) collective-permute-start(bf16[1376,128]{1,0:T(8,128)(2,1)S(1)} %pad_maximum_fusion.4), channel_id=1, source_target_pairs={{0,4},{4,0},{8,12},{12,8},{16,20},{20,16},{24,28},{28,24},{1,5},{5... | collective-permute-start | bytes 1056776 | tf_op jit(solution)/shard_map/ppermute | solution.py:398
  412.0 14.1 %collective-permute-start.67 = (bf16[1376,128]{1,0:T(8,128)(2,1)S(1)}, bf16[1376,128]{1,0:T(8,128)(2,1)S(1)}, u32[]{:S(2)}, u32[]{:S(2)}) collective-permute-start(bf16[1376,128]{1,0:T(8,128)(2,1)S(1)} %pad_maximum_fusion.5), channel_id=1, source_target_pairs={{0,4},{4,0},{8,12},{12,8},{16,20},{20,16},{24,28},{28,24},{1,5},{5... | collective-permute-start | bytes 1056776 | tf_op jit(solution)/shard_map/ppermute | solution.py:398
  426.1 28.2 %collective-permute-start.74 = (bf16[1376,128]{1,0:T(8,128)(2,1)S(1)}, bf16[1376,128]{1,0:T(8,128)(2,1)S(1)}, u32[]{:S(2)}, u32[]{:S(2)}) collective-permute-start(bf16[1376,128]{1,0:T(8,128)(2,1)S(1)} %pad_maximum_fusion.6), channel_id=1, source_target_pairs={{0,4},{4,0},{8,12},{12,8},{16,20},{20,16},{24,28},{28,24},{1,5},{5... | collective-permute-start | bytes 1056776 | tf_op jit(solution)/shard_map/ppermute | solution.py:398
  426.7 27.7 %collective-permute-start.75 = (bf16[1376,128]{1,0:T(8,128)(2,1)S(1)}, bf16[1376,128]{1,0:T(8,128)(2,1)S(1)}, u32[]{:S(2)}, u32[]{:S(2)}) collective-permute-start(bf16[1376,128]{1,0:T(8,128)(2,1)S(1)} %pad_maximum_fusion.7), channel_id=1, source_target_pairs={{0,4},{4,0},{8,12},{12,8},{16,20},{20,16},{24,28},{28,24},{1,5},{5... | collective-permute-start | bytes 1056776 | tf_op jit(solution)/shard_map/ppermute | solution.py:398
  428.2 17.9 %collective-permute-start.69 = (bf16[64,512]{1,0:T(8,128)(2,1)S(1)}, bf16[64,512]{1,0:T(8,128)(2,1)S(1)}, u32[]{:S(2)}, u32[]{:S(2)}) collective-permute-start(bf16[64,512]{1,0:T(8,128)(2,1)S(1)} %get-tuple-element.225), channel_id=1, source_target_pairs={{0,8},{4,12},{8,0},{12,4},{16,24},{20,28},{24,16},{28,20},{1,9},{5... | collective-permute-start | bytes 196616 | tf_op jit(solution)/shard_map/ppermute | solution.py:398
  428.8 18.5 %collective-permute-start.70 = (bf16[64,512]{1,0:T(8,128)(2,1)S(1)}, bf16[64,512]{1,0:T(8,128)(2,1)S(1)}, u32[]{:S(2)}, u32[]{:S(2)}) collective-permute-start(bf16[64,512]{1,0:T(8,128)(2,1)S(1)} %get-tuple-element.226), channel_id=1, source_target_pairs={{0,16},{4,20},{8,24},{12,28},{16,0},{20,4},{24,8},{28,12},{1,17},{... | collective-permute-start | bytes 196616 | tf_op jit(solution)/shard_map/ppermute | solution.py:398
  429.9 17.3 %collective-permute-start.71 = (bf16[64,512]{1,0:T(8,128)(2,1)S(1)}, bf16[64,512]{1,0:T(8,128)(2,1)S(1)}, u32[]{:S(2)}, u32[]{:S(2)}) collective-permute-start(bf16[64,512]{1,0:T(8,128)(2,1)S(1)} %get-tuple-element.227), channel_id=1, source_target_pairs={{0,24},{4,28},{8,16},{12,20},{16,8},{20,12},{24,0},{28,4},{1,25},{... | collective-permute-start | bytes 196616 | tf_op jit(solution)/shard_map/ppermute | solution.py:398
  454.3 18.8 %collective-permute-start.77 = (bf16[64,512]{1,0:T(8,128)(2,1)S(1)}, bf16[64,512]{1,0:T(8,128)(2,1)S(1)}, u32[]{:S(2)}, u32[]{:S(2)}) collective-permute-start(bf16[64,512]{1,0:T(8,128)(2,1)S(1)} %add_convert_fusion.17), channel_id=1, source_target_pairs={{0,24},{4,28},{8,16},{12,20},{16,8},{20,12},{24,0},{28,4},{1,25},{... | collective-permute-start | bytes 196616 | tf_op jit(solution)/shard_map/ppermute | solution.py:398
  456.2 17.0 %collective-permute-start.78 = (bf16[64,512]{1,0:T(8,128)(2,1)S(1)}, bf16[64,512]{1,0:T(8,128)(2,1)S(1)}, u32[]{:S(2)}, u32[]{:S(2)}) collective-permute-start(bf16[64,512]{1,0:T(8,128)(2,1)S(1)} %add_convert_fusion.17), channel_id=1, source_target_pairs={{0,8},{4,12},{8,0},{12,4},{16,24},{20,28},{24,16},{28,20},{1,9},{5... | collective-permute-start | bytes 196616 | tf_op jit(solution)/shard_map/ppermute | solution.py:398
  456.8 16.4 %collective-permute-start.79 = (bf16[64,512]{1,0:T(8,128)(2,1)S(1)}, bf16[64,512]{1,0:T(8,128)(2,1)S(1)}, u32[]{:S(2)}, u32[]{:S(2)}) collective-permute-start(bf16[64,512]{1,0:T(8,128)(2,1)S(1)} %add_convert_fusion.17), channel_id=1, source_target_pairs={{0,16},{4,20},{8,24},{12,28},{16,0},{20,4},{24,8},{28,12},{1,17},{... | collective-permute-start | bytes 196616 | tf_op jit(solution)/shard_map/ppermute | solution.py:398
  458.8 14.4 %collective-permute-start.76 = (bf16[128,1664]{1,0:T(8,128)(2,1)S(1)}, bf16[128,1664]{1,0:T(8,128)(2,1)S(1)}, u32[]{:S(2)}, u32[]{:S(2)}) collective-permute-start(bf16[128,1664]{1,0:T(8,128)(2,1)S(1)} %pad_maximum_fusion.1), channel_id=1, source_target_pairs={{0,4},{4,0},{8,12},{12,8},{16,20},{20,16},{24,28},{28,24},{1,5},{5... | collective-permute-start | bytes 1277960 | tf_op jit(solution)/shard_map/ppermute | solution.py:398
  (73 other events, 443.0 us)
